TPU v7x, 256 devices: a whole 4x4x8 slice. The times are simulated.
256 devices in a mesh: elec: 4 (over z_hi, core), row: 16 (over z_lo, y), col: 4 (over x).
Axes of the slice: x: 4, y: 4, z: 8 (z_hi: 2, z_lo: 4; z = z_hi * 4 + z_lo), core: 2. Of those that a mesh axis runs over, the one named last changes fastest.
Arguments:
- fields: bfloat16 [256, 2, 512, 256], P(('elec', 'row', 'col')), may hold values from -6 to 6
- mirror_phase: float32 [512, 256], replicated, may hold values from -3.140625 to 3.140625
- tile_list: int32 [16, 4, 9, 2], P('row', 'col'), may hold values from -1 to 31, as said below
Outputs:
- csd_tiles: float32 [16, 4, 9, 2, 768, 768], P('row', 'col', None, None, 'elec')
Inputs may be any that keep to these rules, and one draw needn't show every extreme that they name: `tile_list`: each slot of row index r and col index c holds a tile (i, j) of the lower triangle, j <= i, with i equal to r or 31 - r and j congruent to c modulo the number of col indices; every such tile appears in exactly one slot of its r and c, in drawn order; the other slots hold -1 in both entries.
All inputs are finite; a program needn't handle non-finite values.
Results may differ from a plain program's by a relative error of at most 0.012.
Values may be sent and summed in bfloat16 or wider, within the bound.
No kernel may reach another device: no remote copies, remote signals or barrier semaphores. Data moves between devices by JAX's collectives and lax.ppermute only.
A program may use at most 192 MiB of HBM per device.

v0:
```python
import math

import jax
import jax.numpy as jnp
import numpy as np
from jax import lax
from jax.experimental import pallas as pl
from jax.experimental.pallas import tpu as pltpu
from jax.sharding import Mesh, PartitionSpec as P


NX = 512
NY = 256
TILE = 768
QUARTER = 192
SLOTS = 9
ROWS = 24
PEER_ROWS = 288
LANES = 128
AXES = ("zh", "k", "zl", "y", "x")


def dft_parts(length):
    positions = np.arange(length, dtype=np.int32)
    product = positions[:, None] * positions[None, :] % length
    angles = (np.float32(2.0 * math.pi / length) * product.astype(np.float32)).astype(np.float32)
    factor = np.float32(1.0 / math.sqrt(length))
    return np.cos(angles) * factor, np.sin(angles) * factor


def tables():
    bf16 = jnp.bfloat16
    cos_x, sin_x = dft_parts(NX)
    cos_y, sin_y = dft_parts(NY)
    inverse = np.zeros((192, 2 * NX), np.float32)
    turn = np.zeros((192, 192), np.float32)
    order = np.zeros((192, 192), np.float32)

    def place(tile, part, w):
        r, u = (tile, 0) if tile < 16 else (31 - tile, 1)
        return (((r % 4 * 4 + r // 4) * 2 + u) * 2 + part) * 3 + w

    for tile in range(32):
        for w in range(3):
            line = tile * 3 + w
            re, im = place(tile, 0, w), place(tile, 1, w)
            inverse[re] = np.concatenate([cos_x[line], -sin_x[line]])
            inverse[im] = np.concatenate([sin_x[line], cos_x[line]])
            turn[re, im] = -1.0
            turn[im, re] = 1.0
            for part in range(2):
                m, x = divmod(tile, 4)
                target = ((((w * 4 + x) * 2 + m % 2) * 4 + m // 2) * 2) + part
                order[target, place(tile, part, w)] = 1.0
    return [jnp.asarray(a, bf16) for a in (cos_x, sin_x, cos_y, sin_y, inverse, turn, order)]


def dot(a, b):
    return jnp.dot(a, b, preferred_element_type=jnp.float32)


def cos_sin(theta):
    h = theta * 0.5
    s = h * h
    sin_h = h * (1.0 + s * (-1.0 / 6 + s * (1.0 / 120 + s * (-1.0 / 5040 + s * (1.0 / 362880 + s * (-1.0 / 39916800))))))
    cos_h = 1.0 + s * (-0.5 + s * (1.0 / 24 + s * (-1.0 / 720 + s * (1.0 / 40320 + s * (-1.0 / 3628800 + s * (1.0 / 479001600))))))
    return 1.0 - 2.0 * sin_h * sin_h, 2.0 * sin_h * cos_h


def front_kernel(fields, phase, cos_x, sin_x, cos_y, sin_y, inverse, turn, order, *rest):
    bf16 = jnp.bfloat16
    row_out = rest[:4]
    col_out = rest[4:8]
    slab_f, slab_c = rest[8:]
    xr = fields[0, 0]
    xi = fields[0, 1]
    cx = cos_x[...]
    sx = sin_x[...]
    first_r = (dot(cx, xr) + dot(sx, xi)).astype(bf16)
    first_i = (dot(cx, xi) - dot(sx, xr)).astype(bf16)
    cy = cos_y[...]
    sy = sin_y[...]
    turned_r = dot(first_r, cy) + dot(first_i, sy)
    turned_i = dot(first_i, cy) - dot(first_r, sy)
    cos_p, sin_p = cos_sin(phase[...])
    spec_r = (turned_r * cos_p - turned_i * sin_p).astype(bf16)
    spec_i = (turned_r * sin_p + turned_i * cos_p).astype(bf16)
    inv = inverse[...]
    back = (dot(inv[:, :NX], spec_r) + dot(inv[:, NX:], spec_i)).astype(bf16)
    back_turned = dot(turn[...], back).astype(bf16)
    slab = (dot(back, cy) + dot(back_turned, sy)).astype(bf16)
    slab_f[...] = slab.astype(jnp.float32)
    slab_c[...] = dot(order[...], slab)
    x_at = lax.axis_index("x")
    y_at = lax.axis_index("y")
    low = lax.broadcasted_iota(jnp.int32, (8, LANES), 1) < 64
    wide = ((0, 0), (1, 0), (1, 1), (2, 1))
    slim = ((0, 1), (0, 1), (2, 0), (2, 0))
    for o in range(4):
        block = slab_f[pl.ds(pl.multiple_of((y_at ^ o) * 48, 8), 48), :]
        for zl in range(4):
            for u in range(2):
                for h in range(2):
                    at = (zl * 2 + u) * 6
                    to = u * 12 + h * 6
                    row_out[o][zl, to:to + 6, :] = block[at:at + 6, h * LANES:(h + 1) * LANES].astype(bf16)
        xb = (x_at ^ o) * 16
        for q in range(4):
            w, h = wide[q]
            a = slab_c[pl.ds(pl.multiple_of(xb + w * 64, 8), 16), h * LANES:(h + 1) * LANES]
            w, h = slim[q]
            e = slab_c[pl.ds(pl.multiple_of(xb + w * 64, 8), 16), h * LANES:(h + 1) * LANES]
            even, odd = e[:8], e[8:]
            if q % 2 == 0:
                b = jnp.where(low, even, pltpu.roll(odd, 64, 1))
            else:
                b = jnp.where(low, pltpu.roll(even, 64, 1), odd)
            col_out[o][q, 0:16, :] = a.astype(bf16)
            col_out[o][q, 16:24, :] = b.astype(bf16)


def vmem(shape, dtype=jnp.bfloat16):
    return pltpu.VMEM(shape, dtype)


def local_call(kernel, outs, args, scratch=()):
    spec = pl.BlockSpec(memory_space=pltpu.VMEM)
    here = [pltpu.with_memory_space_constraint(a, pltpu.VMEM) for a in args]
    return pl.pallas_call(
        kernel,
        out_shape=[vmem(shape) for shape in outs],
        in_specs=[spec] * len(here),
        out_specs=[spec] * len(outs),
        scratch_shapes=list(scratch),
        compiler_params=pltpu.CompilerParams(vmem_limit_bytes=12 << 20),
    )(*here)


def front(fields, phase):
    return pl.pallas_call(
        front_kernel,
        out_shape=[vmem((4, ROWS, LANES))] * 8,
        out_specs=[pl.BlockSpec(memory_space=pltpu.VMEM)] * 8,
        scratch_shapes=[pltpu.VMEM((192, NY), jnp.float32), pltpu.VMEM((192, NY), jnp.float32)],
        name="front",
    )(fields, phase, *tables())


def pack_kernel(*refs):
    rows = refs[:4]
    cols = refs[4:8]
    outs = refs[8:]
    z_at = lax.axis_index("zh") * 4 + lax.axis_index("zl")
    for d, out in enumerate(outs):
        z = (z_at + d) % 8
        zh = z // 4
        zl = z % 4
        for o in range(4):
            for k in range(2):
                to = o * 48 + k * 24
                out[to:to + 24, :] = cols[o][zh * 2 + k]
            to = 192 + o * 24
            out[to:to + 24, :] = rows[o][zl]


def pack(rows, cols):
    return local_call(pack_kernel, [(PEER_ROWS, LANES)] * 8, [*rows, *cols])


def split_kernel(*refs):
    peers = refs[:8]
    mine, theirs, flat = refs[8:]
    bf16 = jnp.bfloat16
    core = lax.axis_index("k")
    for z in range(8):
        flat[z * PEER_ROWS:(z + 1) * PEER_ROWS, :] = peers[z][...].astype(jnp.float32)

    def pair(at, step):
        return jnp.concatenate(
            [flat[pl.ds(at, 8, stride=PEER_ROWS), :], flat[pl.ds(at + step, 8, stride=PEER_ROWS), :]], axis=0
        ).astype(bf16)

    for out, k in ((mine, core), (theirs, 1 - core)):
        for c in range(2):
            for o in range(0, 4, 2):
                to = (c * 4 + o) * 8
                for j in range(12):
                    out[j, to:to + 16, :] = pair(o * 48 + k * 24 + j * 2 + c, 48)
                for w in range(3):
                    for h in range(2):
                        out[12 + w * 2 + h, to:to + 16, :] = pair(192 + o * 24 + k * 12 + h * 6 + c * 3 + w, 24)


def split(peers):
    return local_call(
        split_kernel,
        [(18, 64, LANES)] * 2,
        peers,
        scratch=[pltpu.VMEM((8 * PEER_ROWS, LANES), jnp.float32)],
    )


def merge_kernel(mine, theirs, row_out, col_out):
    bf16 = jnp.bfloat16
    is_first = lax.axis_index("k") == 0
    for j in range(18):
        a = mine[j].astype(jnp.float32)
        b = theirs[j].astype(jnp.float32)
        first = jnp.where(is_first, a, b).reshape(8, 8, LANES)
        second = jnp.where(is_first, b, a).reshape(8, 8, LANES)
        block = jnp.stack([first, second], axis=1).reshape(LANES, LANES)
        if j < 12:
            col_out[j] = jnp.transpose(block).astype(bf16)
        else:
            lane = (j - 12) * LANES
            row_out[:, lane:lane + LANES] = block.astype(bf16)


def merge(mine, theirs):
    return local_call(merge_kernel, [(LANES, TILE), (12, LANES, LANES)], [mine, theirs])


def join_kernel(r0, r1, r2, r3, out):
    for o, ref in enumerate((r0, r1, r2, r3)):
        for s in range(4):
            for c in range(2):
                to = s * 128 + c * 64 + o * 16
                at = c * 64 + s * 16
                out[to:to + 16, :] = ref[at:at + 16, :]


def join(blocks):
    return local_call(join_kernel, [(512, TILE)], blocks)[0]


def back_kernel(tiles, own, other, c0, c1, c2a, c2b, c3, out, left, ready, sem):
    core = lax.axis_index("k")
    wide_at = pl.multiple_of(core * 64, 64)
    slim_at = pl.multiple_of((1 - core) * 128, 64)
    first = lax.broadcasted_iota(jnp.int32, (LANES, LANES), 1) < 64
    for s in range(4):
        for j in range(12):
            if s == 2:
                block = c2a[j] if j < 6 else c2b[j - 6]
            else:
                block = (c0, c1, None, c3)[s][j]
            moved = pltpu.roll(block.astype(jnp.float32), 64, 1)
            other_block = jnp.where(first, -moved, moved).astype(jnp.bfloat16)
            lanes = slice(s * LANES, (s + 1) * LANES)
            if j < 8:
                m = (j % 4) * 2 + j // 4
                left[m, pl.ds(wide_at, 128), lanes] = block
                left[m, pl.ds(QUARTER + wide_at, 128), lanes] = other_block
            else:
                for par in range(2):
                    m = (j - 8) * 2 + par
                    part = slice(par * 64, par * 64 + 64)
                    left[m, pl.ds(slim_at, 64), lanes] = block[part]
                    left[m, pl.ds(QUARTER + slim_at, 64), lanes] = other_block[part]

    def copy(slot):
        return pltpu.make_async_copy(ready.at[slot], out.at[0, 0, slot], sem.at[slot])

    def one(slot, carry):
        tile_row = tiles[0, 0, slot, 0]
        tile_col = tiles[0, 0, slot, 1]
        m = jnp.maximum(tile_col, 0) // 4
        u = (tile_row >= 16).astype(jnp.int32)

        def write(right):
            res = dot(left[m], right[...]) * 0.0625
            ready[slot, 0] = res[:QUARTER]
            ready[slot, 1] = res[QUARTER:]

        @pl.when(jnp.logical_and(tile_row >= 0, u == core))
        def _():
            write(own)

        @pl.when(jnp.logical_and(tile_row >= 0, u != core))
        def _():
            write(other)

        @pl.when(tile_row < 0)
        def _():
            ready[slot] = jnp.zeros((2, QUARTER, TILE), jnp.float32)

        copy(slot).start()
        return carry

    lax.fori_loop(0, SLOTS, one, 0)
    for slot in range(SLOTS):
        copy(slot).wait()


def back(tiles, *blocks):
    here = [pltpu.with_memory_space_constraint(b, pltpu.VMEM) for b in blocks]
    spec = pl.BlockSpec(memory_space=pltpu.VMEM)
    return pl.pallas_call(
        back_kernel,
        in_specs=[pl.BlockSpec(memory_space=pltpu.SMEM)] + [spec] * len(here),
        out_specs=pl.BlockSpec(memory_space=pl.ANY),
        scratch_shapes=[
            pltpu.VMEM((8, 2 * QUARTER, 512), jnp.bfloat16),
            pltpu.VMEM((SLOTS, 2, QUARTER, TILE), jnp.float32),
            pltpu.SemaphoreType.DMA((SLOTS,)),
        ],
        compiler_params=pltpu.CompilerParams(vmem_limit_bytes=28 << 20),
        out_shape=jax.ShapeDtypeStruct((1, 1, SLOTS, 2, QUARTER, TILE), jnp.float32),
        name="back",
    )(tiles, *here)


def swap(value, axis, bits):
    return lax.ppermute(value, axis, [(i, i ^ bits) for i in range(lax.axis_size(axis))])


def shift(value, by):
    return lax.ppermute(value, ("zh", "zl"), [(i, (i + by) % 8) for i in range(8)])


def body(fields, mirror_phase, tile_list):
    pieces = front(fields, mirror_phase)
    rows, cols = pieces[:4], pieces[4:]
    cols = [cols[0]] + [swap(cols[o], "x", o) for o in (1, 2, 3)]
    rows = [rows[0]] + [swap(rows[o], "y", o) for o in (1, 2, 3)]
    peers = pack(rows, cols)
    peers = [peers[0]] + [shift(peers[o], o) for o in range(1, 8)]
    mine, theirs = split(peers)
    theirs = swap(theirs, "k", 1)
    r0, c0 = merge(mine, theirs)
    c1 = swap(c0, "y", 1)
    c3 = swap(c0, "y", 3)
    r1 = swap(r0, "x", 1)
    r3 = swap(r0, "x", 3)
    c2a = swap(c3[:6], "y", 1)
    c2b = swap(c1[6:], "y", 3)
    r2 = swap(r3, "x", 1)
    own = join([r0, r1, r2, r3])
    other = swap(own, "k", 1)
    return back(tile_list, own, other, c0, c1, c2a, c2b, c3)


def solution(mesh):
    fine = Mesh(mesh.devices.reshape(2, 2, 4, 4, 4), AXES)
    in_specs = (P(AXES, None, None, None), P(), P(("zl", "y"), "x", None, None))
    out_specs = P(("zl", "y"), "x", None, None, ("zh", "k"), None)

    return jax.shard_map(body, mesh=fine, in_specs=in_specs, out_specs=out_specs, check_vma=False)
```

profile of v0, /device:TPU:1, one launch (start us, length us, event | category | flops | bytes accessed | tf_op | source)
XLA Modules:
  0.0 87.5 jit_solution(15174508740537198783)
XLA Ops:
  0.0 4.0 %front.1 = (bf16[4,24,128]{2,1,0:T(8,128)(2,1)S(1)}, bf16[4,24,128]{2,1,0:T(8,128)(2,1)S(1)}, bf16[4,24,128]{2,1,0:T(8,128)(2,1)S(1)}, bf16[4,24,128]{2,1,0:T(8,...) custom-call(bf16[1,2,512,256]{3,2,1,0:T(8,128)(2,1)} %fields.1, ...), custom_call_target="tpu_custom_call" | custom-call | tf_op jit(solution)/shard_map/front/pallas_call | solution.py:140
  4.0 2.2 %collective-permute-start = (bf16[4,24,128]{2,1,0:T(8,128)(2,1)S(1)}, bf16[4,24,128]{2,1,0:T(8,128)(2,1)S(1)}, u32[]{:S(2)}, u32[]{:S(2)}) collective-permute-start(bf16[4,24,128]{2,1,0:T(8,128)(2,1)S(1)} %get-tuple-element.26), channel_id=1, source_target_pairs={{0,4},{4,0},{8,12},{12,8},{1,5},{5,1},{9,13},{13,9},{2,6},{6,2},{1... | collective-permute-start | bytes 73736 | tf_op jit(solution)/shard_map/ppermute | solution.py:314
  6.2 2.6 %collective-permute-start.1 = (bf16[4,24,128]{2,1,0:T(8,128)(2,1)S(1)}, bf16[4,24,128]{2,1,0:T(8,128)(2,1)S(1)}, u32[]{:S(2)}, u32[]{:S(2)}) collective-permute-start(bf16[4,24,128]{2,1,0:T(8,128)(2,1)S(1)} %get-tuple-element.27), channel_id=1, source_target_pairs={{0,8},{4,12},{8,0},{12,4},{1,9},{5,13},{9,1},{13,5},{2,10},{6,14},... | collective-permute-start | bytes 73736 | tf_op jit(solution)/shard_map/ppermute | solution.py:314
  8.8 0.0 collective-permute-start.2
  8.9 1.2 %collective-permute-start.3 = (bf16[4,24,128]{2,1,0:T(8,128)(2,1)S(1)}, bf16[4,24,128]{2,1,0:T(8,128)(2,1)S(1)}, u32[]{:S(2)}, u32[]{:S(2)}) collective-permute-start(bf16[4,24,128]{2,1,0:T(8,128)(2,1)S(1)} %get-tuple-element.30), channel_id=1, source_target_pairs={{0,1},{1,0},{2,3},{3,2},{4,5},{5,4},{6,7},{7,6},{8,9},{9,8},{10,11... | collective-permute-start | bytes 73736 | tf_op jit(solution)/shard_map/ppermute | solution.py:314
  10.1 2.5 %collective-permute-start.4 = (bf16[4,24,128]{2,1,0:T(8,128)(2,1)S(1)}, bf16[4,24,128]{2,1,0:T(8,128)(2,1)S(1)}, u32[]{:S(2)}, u32[]{:S(2)}) collective-permute-start(bf16[4,24,128]{2,1,0:T(8,128)(2,1)S(1)} %get-tuple-element.31), channel_id=1, source_target_pairs={{0,2},{1,3},{2,0},{3,1},{4,6},{5,7},{6,4},{7,5},{8,10},{9,11},{10,... | collective-permute-start | bytes 73736 | tf_op jit(solution)/shard_map/ppermute | solution.py:314
  12.5 0.0 collective-permute-done.refs_1_
  12.5 0.2 collective-permute-start.5
  12.7 0.0 collective-permute-done.1.refs_2_
  12.7 0.0 collective-permute-done.2.refs_3_
  12.7 0.0 collective-permute-done.3.refs_5_
  12.7 1.5 %collective-permute-done.4.refs_6_ = bf16[4,24,128]{2,1,0:T(8,128)(2,1)S(1)} collective-permute-done((bf16[4,24,128]{2,1,0:T(8,128)(2,1)S(1)}, bf16[4,24,128]{2,1,0:T(8,128)(2,1)S(1)}, u32[]{:S(2)}, u32[]{:S(2)}) %collective-permute-start.4) | collective-permute-done | bytes 24608 | tf_op jit(solution)/shard_map/ppermute | solution.py:314
  14.2 2.5 %collective-permute-done.5.refs_7_ = bf16[4,24,128]{2,1,0:T(8,128)(2,1)S(1)} collective-permute-done((bf16[4,24,128]{2,1,0:T(8,128)(2,1)S(1)}, bf16[4,24,128]{2,1,0:T(8,128)(2,1)S(1)}, u32[]{:S(2)}, u32[]{:S(2)}) %collective-permute-start.5) | collective-permute-done | bytes 24608 | tf_op jit(solution)/shard_map/ppermute | solution.py:314
  16.7 0.1 shard_map.100
  16.8 1.7 %collective-permute-start.6 = (bf16[288,128]{1,0:T(8,128)(2,1)S(1)}, bf16[288,128]{1,0:T(8,128)(2,1)S(1)}, u32[]{:S(2)}, u32[]{:S(2)}) collective-permute-start(bf16[288,128]{1,0:T(8,128)(2,1)S(1)} %get-tuple-element.34), channel_id=1, source_target_pairs={{0,16},{16,32},{32,48},{48,128},{128,144},{144,160},{160,176},{176... | collective-permute-start | bytes 221192 | tf_op jit(solution)/shard_map/ppermute | solution.py:318
  18.5 3.0 %collective-permute-start.7 = (bf16[288,128]{1,0:T(8,128)(2,1)S(1)}, bf16[288,128]{1,0:T(8,128)(2,1)S(1)}, u32[]{:S(2)}, u32[]{:S(2)}) collective-permute-start(bf16[288,128]{1,0:T(8,128)(2,1)S(1)} %get-tuple-element.35), channel_id=1, source_target_pairs={{0,32},{16,48},{32,128},{48,144},{128,160},{144,176},{160,0},{176,... | collective-permute-start | bytes 221192 | tf_op jit(solution)/shard_map/ppermute | solution.py:318
  21.5 3.8 %collective-permute-start.8 = (bf16[288,128]{1,0:T(8,128)(2,1)S(1)}, bf16[288,128]{1,0:T(8,128)(2,1)S(1)}, u32[]{:S(2)}, u32[]{:S(2)}) collective-permute-start(bf16[288,128]{1,0:T(8,128)(2,1)S(1)} %get-tuple-element.36), channel_id=1, source_target_pairs={{0,48},{16,128},{32,144},{48,160},{128,176},{144,0},{160,16},{176,... | collective-permute-start | bytes 221192 | tf_op jit(solution)/shard_map/ppermute | solution.py:318
  25.3 0.5 collective-permute-start.9
  25.7 4.5 %collective-permute-start.10 = (bf16[288,128]{1,0:T(8,128)(2,1)S(1)}, bf16[288,128]{1,0:T(8,128)(2,1)S(1)}, u32[]{:S(2)}, u32[]{:S(2)}) collective-permute-start(bf16[288,128]{1,0:T(8,128)(2,1)S(1)} %get-tuple-element.38), channel_id=1, source_target_pairs={{0,144},{16,160},{32,176},{48,0},{128,16},{144,32},{160,48},{176,1... | collective-permute-start | bytes 221192 | tf_op jit(solution)/shard_map/ppermute | solution.py:318
  30.2 0.0 collective-permute-done.6.refs_1_
  30.2 2.4 %collective-permute-start.11 = (bf16[288,128]{1,0:T(8,128)(2,1)S(1)}, bf16[288,128]{1,0:T(8,128)(2,1)S(1)}, u32[]{:S(2)}, u32[]{:S(2)}) collective-permute-start(bf16[288,128]{1,0:T(8,128)(2,1)S(1)} %get-tuple-element.39), channel_id=1, source_target_pairs={{0,160},{16,176},{32,0},{48,16},{128,32},{144,48},{160,128},{176,1... | collective-permute-start | bytes 221192 | tf_op jit(solution)/shard_map/ppermute | solution.py:318
  32.6 0.0 collective-permute-done.7.refs_2_
  32.6 0.7 collective-permute-start.12
  33.3 0.0 collective-permute-done.8.refs_3_
  33.3 1.7 %collective-permute-done.9.refs_4_ = bf16[288,128]{1,0:T(8,128)(2,1)S(1)} collective-permute-done((bf16[288,128]{1,0:T(8,128)(2,1)S(1)}, bf16[288,128]{1,0:T(8,128)(2,1)S(1)}, u32[]{:S(2)}, u32[]{:S(2)}) %collective-permute-start.9) | collective-permute-done | bytes 73760 | tf_op jit(solution)/shard_map/ppermute | solution.py:318
  35.0 0.0 collective-permute-done.10.refs_5_
  35.0 5.2 %collective-permute-done.11.refs_6_ = bf16[288,128]{1,0:T(8,128)(2,1)S(1)} collective-permute-done((bf16[288,128]{1,0:T(8,128)(2,1)S(1)}, bf16[288,128]{1,0:T(8,128)(2,1)S(1)}, u32[]{:S(2)}, u32[]{:S(2)}) %collective-permute-start.11) | collective-permute-done | bytes 73760 | tf_op jit(solution)/shard_map/ppermute | solution.py:318
  40.2 1.6 %collective-permute-done.12.refs_7_ = bf16[288,128]{1,0:T(8,128)(2,1)S(1)} collective-permute-done((bf16[288,128]{1,0:T(8,128)(2,1)S(1)}, bf16[288,128]{1,0:T(8,128)(2,1)S(1)}, u32[]{:S(2)}, u32[]{:S(2)}) %collective-permute-start.12) | collective-permute-done | bytes 73760 | tf_op jit(solution)/shard_map/ppermute | solution.py:318
  41.8 0.7 shard_map.101
  42.5 2.0 %collective-permute-start.13 = (bf16[18,64,128]{2,1,0:T(8,128)(2,1)S(1)}, bf16[18,64,128]{2,1,0:T(8,128)(2,1)S(1)}, u32[]{:S(2)}, u32[]{:S(2)}) collective-permute-start(bf16[18,64,128]{2,1,0:T(8,128)(2,1)S(1)} %get-tuple-element.42), channel_id=1, source_target_pairs={{0,64},{64,0},{1,65},{65,1},{2,66},{66,2},{3,67},{67,3},{4,68},{68... | collective-permute-start | bytes 884744 | tf_op jit(solution)/shard_map/ppermute | solution.py:314
  44.5 1.2 %collective-permute-done.13.theirs = bf16[18,64,128]{2,1,0:T(8,128)(2,1)S(1)} collective-permute-done((bf16[18,64,128]{2,1,0:T(8,128)(2,1)S(1)}, bf16[18,64,128]{2,1,0:T(8,128)(2,1)S(1)}, u32[]{:S(2)}, u32[]{:S(2)}) %collective-permute-start.13) | collective-permute-done | bytes 294944 | tf_op jit(solution)/shard_map/ppermute | solution.py:314
  45.7 0.2 shard_map.102
  45.9 0.3 collective-permute-start.15
  46.2 0.1 collective-permute-start.14
  46.3 7.2 %collective-permute-done.15.r3 = bf16[128,768]{1,0:T(8,128)(2,1)S(1)} collective-permute-done((bf16[128,768]{1,0:T(8,128)(2,1)S(1)}, bf16[128,768]{1,0:T(8,128)(2,1)S(1)}, u32[]{:S(2)}, u32[]{:S(2)}) %collective-permute-start.15) | collective-permute-done | bytes 196640 | tf_op jit(solution)/shard_map/ppermute | solution.py:314
  53.5 5.2 %collective-permute-done.16.r2 = bf16[128,768]{1,0:T(8,128)(2,1)S(1)} collective-permute-done((bf16[128,768]{1,0:T(8,128)(2,1)S(1)}, bf16[128,768]{1,0:T(8,128)(2,1)S(1)}, u32[]{:S(2)}, u32[]{:S(2)}) %collective-permute-start.16) | collective-permute-done | bytes 196640 | tf_op jit(solution)/shard_map/ppermute | solution.py:314
  58.7 0.1 shard_map.103.own
  58.8 2.2 %collective-permute-start.17 = (bf16[512,768]{1,0:T(8,128)(2,1)S(1)}, bf16[512,768]{1,0:T(8,128)(2,1)S(1)}, u32[]{:S(2)}, u32[]{:S(2)}) collective-permute-start(bf16[512,768]{1,0:T(8,128)(2,1)S(1)} %shard_map.103.own), channel_id=1, source_target_pairs={{0,64},{64,0},{1,65},{65,1},{2,66},{66,2},{3,67},{67,3},{4,68},{68... | collective-permute-start | bytes 2359304 | tf_op jit(solution)/shard_map/ppermute | solution.py:314
  60.9 2.7 %collective-permute-start.19 = (bf16[12,128,128]{2,1,0:T(8,128)(2,1)S(1)}, bf16[12,128,128]{2,1,0:T(8,128)(2,1)S(1)}, u32[]{:S(2)}, u32[]{:S(2)}) collective-permute-start(bf16[12,128,128]{2,1,0:T(8,128)(2,1)S(1)} %get-tuple-element.44.c0), channel_id=1, source_target_pairs={{0,12},{4,8},{8,4},{12,0},{1,13},{5,9},{9,5},{13,1},{2,14},{6,10},... | collective-permute-start | bytes 1179656 | tf_op jit(solution)/shard_map/ppermute | solution.py:314
  63.7 9.2 %collective-permute-done.19.c3 = bf16[12,128,128]{2,1,0:T(8,128)(2,1)S(1)} collective-permute-done((bf16[12,128,128]{2,1,0:T(8,128)(2,1)S(1)}, bf16[12,128,128]{2,1,0:T(8,128)(2,1)S(1)}, u32[]{:S(2)}, u32[]{:S(2)}) %collective-permute-start.19) | collective-permute-done | bytes 393248 | tf_op jit(solution)/shard_map/ppermute | solution.py:314
  72.9 0.1 collective-permute-start.20
  73.0 1.0 %collective-permute-done.18.c1 = bf16[12,128,128]{2,1,0:T(8,128)(2,1)S(1)} collective-permute-done((bf16[12,128,128]{2,1,0:T(8,128)(2,1)S(1)}, bf16[12,128,128]{2,1,0:T(8,128)(2,1)S(1)}, u32[]{:S(2)}, u32[]{:S(2)}) %collective-permute-start.18) | collective-permute-done | bytes 393248 | tf_op jit(solution)/shard_map/ppermute | solution.py:314
  74.0 1.7 %collective-permute-start.21 = (bf16[6,128,128]{2,1,0:T(8,128)(2,1)S(1)}, bf16[6,128,128]{2,1,0:T(8,128)(2,1)S(1)}, u32[]{:S(2)}, u32[]{:S(2)}) collective-permute-start(bf16[6,128,128]{2,1,0:T(8,128)(2,1)S(1)} %slice.9), channel_id=1, source_target_pairs={{0,12},{4,8},{8,4},{12,0},{1,13},{5,9},{9,5},{13,1},{2,14},{6,10},... | collective-permute-start | bytes 589832 | tf_op jit(solution)/shard_map/ppermute | solution.py:314
  75.7 0.8 copy.11.tiles
  76.5 2.0 %collective-permute-done.20.c2a = bf16[6,128,128]{2,1,0:T(8,128)(2,1)S(1)} collective-permute-done((bf16[6,128,128]{2,1,0:T(8,128)(2,1)S(1)}, bf16[6,128,128]{2,1,0:T(8,128)(2,1)S(1)}, u32[]{:S(2)}, u32[]{:S(2)}) %collective-permute-start.20) | collective-permute-done | bytes 196640 | tf_op jit(solution)/shard_map/ppermute | solution.py:314
  78.5 2.0 %collective-permute-done.21.c2b = bf16[6,128,128]{2,1,0:T(8,128)(2,1)S(1)} collective-permute-done((bf16[6,128,128]{2,1,0:T(8,128)(2,1)S(1)}, bf16[6,128,128]{2,1,0:T(8,128)(2,1)S(1)}, u32[]{:S(2)}, u32[]{:S(2)}) %collective-permute-start.21) | collective-permute-done | bytes 196640 | tf_op jit(solution)/shard_map/ppermute | solution.py:314
  80.5 0.0 collective-permute-done.17.other
  80.5 6.9 %back.1 = f32[1,1,9,2,192,768]{5,4,3,2,1,0:T(8,128)} custom-call(s32[1,1,9,2]{3,2,1,0:T(8,128)S(1)} %copy.11.tiles, bf16[512,768]{1,0:T(8,128)(2,1)S(1)} %shard_map.103.own, bf16[512,768]{1,0:T(8,128)(2,1)S(1)} %collective-permute-done.17.other, bf16[12,128,128]{2,1,0:T(8,128)(2,1)S(1)} %get-tuple-element.44.c0, ...), custom_call_target="tpu_custom_call" | custom-call | tf_op jit(solution)/shard_map/back/pallas_call | solution.py:298
  (5 shorter events, 0.0 us)
Async XLA Ops:
  4.0 8.5 %collective-permute-start = (bf16[4,24,128]{2,1,0:T(8,128)(2,1)S(1)}, bf16[4,24,128]{2,1,0:T(8,128)(2,1)S(1)}, u32[]{:S(2)}, u32[]{:S(2)}) collective-permute-start(bf16[4,24,128]{2,1,0:T(8,128)(2,1)S(1)} %get-tuple-element.26), channel_id=1, source_target_pairs={{0,4},{4,0},{8,12},{12,8},{1,5},{5,1},{9,13},{13,9},{2,6},{6,2},{1... | collective-permute-start | bytes 73736 | tf_op jit(solution)/shard_map/ppermute | solution.py:314
  6.2 6.5 %collective-permute-start.1 = (bf16[4,24,128]{2,1,0:T(8,128)(2,1)S(1)}, bf16[4,24,128]{2,1,0:T(8,128)(2,1)S(1)}, u32[]{:S(2)}, u32[]{:S(2)}) collective-permute-start(bf16[4,24,128]{2,1,0:T(8,128)(2,1)S(1)} %get-tuple-element.27), channel_id=1, source_target_pairs={{0,8},{4,12},{8,0},{12,4},{1,9},{5,13},{9,1},{13,5},{2,10},{6,14},... | collective-permute-start | bytes 73736 | tf_op jit(solution)/shard_map/ppermute | solution.py:314
  8.8 3.9 %collective-permute-start.2 = (bf16[4,24,128]{2,1,0:T(8,128)(2,1)S(1)}, bf16[4,24,128]{2,1,0:T(8,128)(2,1)S(1)}, u32[]{:S(2)}, u32[]{:S(2)}) collective-permute-start(bf16[4,24,128]{2,1,0:T(8,128)(2,1)S(1)} %get-tuple-element.28), channel_id=1, source_target_pairs={{0,12},{4,8},{8,4},{12,0},{1,13},{5,9},{9,5},{13,1},{2,14},{6,10},... | collective-permute-start | bytes 73736 | tf_op jit(solution)/shard_map/ppermute | solution.py:314
  8.9 3.9 %collective-permute-start.3 = (bf16[4,24,128]{2,1,0:T(8,128)(2,1)S(1)}, bf16[4,24,128]{2,1,0:T(8,128)(2,1)S(1)}, u32[]{:S(2)}, u32[]{:S(2)}) collective-permute-start(bf16[4,24,128]{2,1,0:T(8,128)(2,1)S(1)} %get-tuple-element.30), channel_id=1, source_target_pairs={{0,1},{1,0},{2,3},{3,2},{4,5},{5,4},{6,7},{7,6},{8,9},{9,8},{10,11... | collective-permute-start | bytes 73736 | tf_op jit(solution)/shard_map/ppermute | solution.py:314
  10.1 4.2 %collective-permute-start.4 = (bf16[4,24,128]{2,1,0:T(8,128)(2,1)S(1)}, bf16[4,24,128]{2,1,0:T(8,128)(2,1)S(1)}, u32[]{:S(2)}, u32[]{:S(2)}) collective-permute-start(bf16[4,24,128]{2,1,0:T(8,128)(2,1)S(1)} %get-tuple-element.31), channel_id=1, source_target_pairs={{0,2},{1,3},{2,0},{3,1},{4,6},{5,7},{6,4},{7,5},{8,10},{9,11},{10,... | collective-permute-start | bytes 73736 | tf_op jit(solution)/shard_map/ppermute | solution.py:314
  12.5 4.2 %collective-permute-start.5 = (bf16[4,24,128]{2,1,0:T(8,128)(2,1)S(1)}, bf16[4,24,128]{2,1,0:T(8,128)(2,1)S(1)}, u32[]{:S(2)}, u32[]{:S(2)}) collective-permute-start(bf16[4,24,128]{2,1,0:T(8,128)(2,1)S(1)} %get-tuple-element.32), channel_id=1, source_target_pairs={{0,3},{1,2},{2,1},{3,0},{4,7},{5,6},{6,5},{7,4},{8,11},{9,10},{10,... | collective-permute-start | bytes 73736 | tf_op jit(solution)/shard_map/ppermute | solution.py:314
  16.8 13.4 %collective-permute-start.6 = (bf16[288,128]{1,0:T(8,128)(2,1)S(1)}, bf16[288,128]{1,0:T(8,128)(2,1)S(1)}, u32[]{:S(2)}, u32[]{:S(2)}) collective-permute-start(bf16[288,128]{1,0:T(8,128)(2,1)S(1)} %get-tuple-element.34), channel_id=1, source_target_pairs={{0,16},{16,32},{32,48},{48,128},{128,144},{144,160},{160,176},{176... | collective-permute-start | bytes 221192 | tf_op jit(solution)/shard_map/ppermute | solution.py:318
  18.5 14.1 %collective-permute-start.7 = (bf16[288,128]{1,0:T(8,128)(2,1)S(1)}, bf16[288,128]{1,0:T(8,128)(2,1)S(1)}, u32[]{:S(2)}, u32[]{:S(2)}) collective-permute-start(bf16[288,128]{1,0:T(8,128)(2,1)S(1)} %get-tuple-element.35), channel_id=1, source_target_pairs={{0,32},{16,48},{32,128},{48,144},{128,160},{144,176},{160,0},{176,... | collective-permute-start | bytes 221192 | tf_op jit(solution)/shard_map/ppermute | solution.py:318
  21.5 11.8 %collective-permute-start.8 = (bf16[288,128]{1,0:T(8,128)(2,1)S(1)}, bf16[288,128]{1,0:T(8,128)(2,1)S(1)}, u32[]{:S(2)}, u32[]{:S(2)}) collective-permute-start(bf16[288,128]{1,0:T(8,128)(2,1)S(1)} %get-tuple-element.36), channel_id=1, source_target_pairs={{0,48},{16,128},{32,144},{48,160},{128,176},{144,0},{160,16},{176,... | collective-permute-start | bytes 221192 | tf_op jit(solution)/shard_map/ppermute | solution.py:318
  25.3 9.7 %collective-permute-start.9 = (bf16[288,128]{1,0:T(8,128)(2,1)S(1)}, bf16[288,128]{1,0:T(8,128)(2,1)S(1)}, u32[]{:S(2)}, u32[]{:S(2)}) collective-permute-start(bf16[288,128]{1,0:T(8,128)(2,1)S(1)} %get-tuple-element.37), channel_id=1, source_target_pairs={{0,128},{16,144},{32,160},{48,176},{128,0},{144,16},{160,32},{176,... | collective-permute-start | bytes 221192 | tf_op jit(solution)/shard_map/ppermute | solution.py:318
  25.7 9.3 %collective-permute-start.10 = (bf16[288,128]{1,0:T(8,128)(2,1)S(1)}, bf16[288,128]{1,0:T(8,128)(2,1)S(1)}, u32[]{:S(2)}, u32[]{:S(2)}) collective-permute-start(bf16[288,128]{1,0:T(8,128)(2,1)S(1)} %get-tuple-element.38), channel_id=1, source_target_pairs={{0,144},{16,160},{32,176},{48,0},{128,16},{144,32},{160,48},{176,1... | collective-permute-start | bytes 221192 | tf_op jit(solution)/shard_map/ppermute | solution.py:318
  30.2 10.0 %collective-permute-start.11 = (bf16[288,128]{1,0:T(8,128)(2,1)S(1)}, bf16[288,128]{1,0:T(8,128)(2,1)S(1)}, u32[]{:S(2)}, u32[]{:S(2)}) collective-permute-start(bf16[288,128]{1,0:T(8,128)(2,1)S(1)} %get-tuple-element.39), channel_id=1, source_target_pairs={{0,160},{16,176},{32,0},{48,16},{128,32},{144,48},{160,128},{176,1... | collective-permute-start | bytes 221192 | tf_op jit(solution)/shard_map/ppermute | solution.py:318
  32.6 9.2 %collective-permute-start.12 = (bf16[288,128]{1,0:T(8,128)(2,1)S(1)}, bf16[288,128]{1,0:T(8,128)(2,1)S(1)}, u32[]{:S(2)}, u32[]{:S(2)}) collective-permute-start(bf16[288,128]{1,0:T(8,128)(2,1)S(1)} %get-tuple-element.40), channel_id=1, source_target_pairs={{0,176},{16,0},{32,16},{48,32},{128,48},{144,128},{160,144},{176,1... | collective-permute-start | bytes 221192 | tf_op jit(solution)/shard_map/ppermute | solution.py:318
  42.5 3.2 %collective-permute-start.13 = (bf16[18,64,128]{2,1,0:T(8,128)(2,1)S(1)}, bf16[18,64,128]{2,1,0:T(8,128)(2,1)S(1)}, u32[]{:S(2)}, u32[]{:S(2)}) collective-permute-start(bf16[18,64,128]{2,1,0:T(8,128)(2,1)S(1)} %get-tuple-element.42), channel_id=1, source_target_pairs={{0,64},{64,0},{1,65},{65,1},{2,66},{66,2},{3,67},{67,3},{4,68},{68... | collective-permute-start | bytes 884744 | tf_op jit(solution)/shard_map/ppermute | solution.py:314
  45.9 7.6 %collective-permute-start.15 = (bf16[128,768]{1,0:T(8,128)(2,1)S(1)}, bf16[128,768]{1,0:T(8,128)(2,1)S(1)}, u32[]{:S(2)}, u32[]{:S(2)}) collective-permute-start(bf16[128,768]{1,0:T(8,128)(2,1)S(1)} %get-tuple-element.43.r0), channel_id=1, source_target_pairs={{0,3},{1,2},{2,1},{3,0},{4,7},{5,6},{6,5},{7,4},{8,11},{9,10},{10,... | collective-permute-start | bytes 589832 | tf_op jit(solution)/shard_map/ppermute | solution.py:314
  46.2 7.3 %collective-permute-start.14 = (bf16[128,768]{1,0:T(8,128)(2,1)S(1)}, bf16[128,768]{1,0:T(8,128)(2,1)S(1)}, u32[]{:S(2)}, u32[]{:S(2)}) collective-permute-start(bf16[128,768]{1,0:T(8,128)(2,1)S(1)} %get-tuple-element.43.r0), channel_id=1, source_target_pairs={{0,1},{1,0},{2,3},{3,2},{4,5},{5,4},{6,7},{7,6},{8,9},{9,8},{10,11... | collective-permute-start | bytes 589832 | tf_op jit(solution)/shard_map/ppermute | solution.py:314
  53.5 5.2 %collective-permute-start.16 = (bf16[128,768]{1,0:T(8,128)(2,1)S(1)}, bf16[128,768]{1,0:T(8,128)(2,1)S(1)}, u32[]{:S(2)}, u32[]{:S(2)}) collective-permute-start(bf16[128,768]{1,0:T(8,128)(2,1)S(1)} %collective-permute-done.15.r3), channel_id=1, source_target_pairs={{0,1},{1,0},{2,3},{3,2},{4,5},{5,4},{6,7},{7,6},{8,9},{9,8},{10,11... | collective-permute-start | bytes 589832 | tf_op jit(solution)/shard_map/ppermute | solution.py:314
  58.8 21.7 %collective-permute-start.17 = (bf16[512,768]{1,0:T(8,128)(2,1)S(1)}, bf16[512,768]{1,0:T(8,128)(2,1)S(1)}, u32[]{:S(2)}, u32[]{:S(2)}) collective-permute-start(bf16[512,768]{1,0:T(8,128)(2,1)S(1)} %shard_map.103.own), channel_id=1, source_target_pairs={{0,64},{64,0},{1,65},{65,1},{2,66},{66,2},{3,67},{67,3},{4,68},{68... | collective-permute-start | bytes 2359304 | tf_op jit(solution)/shard_map/ppermute | solution.py:314
  60.9 11.9 %collective-permute-start.19 = (bf16[12,128,128]{2,1,0:T(8,128)(2,1)S(1)}, bf16[12,128,128]{2,1,0:T(8,128)(2,1)S(1)}, u32[]{:S(2)}, u32[]{:S(2)}) collective-permute-start(bf16[12,128,128]{2,1,0:T(8,128)(2,1)S(1)} %get-tuple-element.44.c0), channel_id=1, source_target_pairs={{0,12},{4,8},{8,4},{12,0},{1,13},{5,9},{9,5},{13,1},{2,14},{6,10},... | collective-permute-start | bytes 1179656 | tf_op jit(solution)/shard_map/ppermute | solution.py:314
  63.7 10.3 %collective-permute-start.18 = (bf16[12,128,128]{2,1,0:T(8,128)(2,1)S(1)}, bf16[12,128,128]{2,1,0:T(8,128)(2,1)S(1)}, u32[]{:S(2)}, u32[]{:S(2)}) collective-permute-start(bf16[12,128,128]{2,1,0:T(8,128)(2,1)S(1)} %get-tuple-element.44.c0), channel_id=1, source_target_pairs={{0,4},{4,0},{8,12},{12,8},{1,5},{5,1},{9,13},{13,9},{2,6},{6,2},{1... | collective-permute-start | bytes 1179656 | tf_op jit(solution)/shard_map/ppermute | solution.py:314
  72.9 5.6 %collective-permute-start.20 = (bf16[6,128,128]{2,1,0:T(8,128)(2,1)S(1)}, bf16[6,128,128]{2,1,0:T(8,128)(2,1)S(1)}, u32[]{:S(2)}, u32[]{:S(2)}) collective-permute-start(bf16[6,128,128]{2,1,0:T(8,128)(2,1)S(1)} %slice.8), channel_id=1, source_target_pairs={{0,4},{4,0},{8,12},{12,8},{1,5},{5,1},{9,13},{13,9},{2,6},{6,2},{1... | collective-permute-start | bytes 589832 | tf_op jit(solution)/shard_map/ppermute | solution.py:314
  74.0 6.5 %collective-permute-start.21 = (bf16[6,128,128]{2,1,0:T(8,128)(2,1)S(1)}, bf16[6,128,128]{2,1,0:T(8,128)(2,1)S(1)}, u32[]{:S(2)}, u32[]{:S(2)}) collective-permute-start(bf16[6,128,128]{2,1,0:T(8,128)(2,1)S(1)} %slice.9), channel_id=1, source_target_pairs={{0,12},{4,8},{8,4},{12,0},{1,13},{5,9},{9,5},{13,1},{2,14},{6,10},... | collective-permute-start | bytes 589832 | tf_op jit(solution)/shard_map/ppermute | solution.py:314
where the time goes:
time: 87.7 us; the launch traced here: 87.5 us
  waiting for transfers between devices  40.3 us (46%)
  starting transfers between devices  34.3 us (39%)
  Pallas kernels  11.9 us (14%)
    ppermute x15, waiting for transfers between devices, swap(): lax.ppermute(value, axis, [(i, i ^ bits) for i in range(lax.axis_size(axi...  31.8 us
    ppermute x15, starting transfers between devices, swap(): lax.ppermute(value, axis, [(i, i ^ bits) for i in range(lax.axis_size(axi...  17.8 us
    ppermute x7, starting transfers between devices, shift(): lax.ppermute(value, ('zh', 'zl'), [(i, (i + by) % 8) for i in range(8)])  16.5 us
    ppermute x7, waiting for transfers between devices, shift(): lax.ppermute(value, ('zh', 'zl'), [(i, (i + by) % 8) for i in range(8)])  8.44 us
    pallas_call x1, Pallas kernels, back(): pl.pallas_call(back_kernel, in_specs=[pl.BlockSpec(memory_space=pltpu.SME...  6.87 us
    pallas_call x1, Pallas kernels, front(): pl.pallas_call(front_kernel, out_shape=[vmem((4, ROWS, LANES))] * 8, out_...  4.02 us
  transfers between devices with their start and end apart: 22, of which 12 were waited for; matrix products, arithmetic and copies ran while one was open for 1% of the time, Pallas kernels for 0%

commit v1 on v0

--- a/solution.py
+++ b/solution.py
@@ -67,11 +67,8 @@
     return 1.0 - 2.0 * sin_h * sin_h, 2.0 * sin_h * cos_h
 
 
-def front_kernel(fields, phase, cos_x, sin_x, cos_y, sin_y, inverse, turn, order, *rest):
+def front_kernel(fields, phase, cos_x, sin_x, cos_y, sin_y, inverse, turn, order, keep, give, slab_f, slab_c):
     bf16 = jnp.bfloat16
-    row_out = rest[:4]
-    col_out = rest[4:8]
-    slab_f, slab_c = rest[8:]
     xr = fields[0, 0]
     xi = fields[0, 1]
     cx = cos_x[...]
@@ -96,27 +93,43 @@
     low = lax.broadcasted_iota(jnp.int32, (8, LANES), 1) < 64
     wide = ((0, 0), (1, 0), (1, 1), (2, 1))
     slim = ((0, 1), (0, 1), (2, 0), (2, 0))
-    for o in range(4):
-        block = slab_f[pl.ds(pl.multiple_of((y_at ^ o) * 48, 8), 48), :]
-        for zl in range(4):
-            for u in range(2):
-                for h in range(2):
-                    at = (zl * 2 + u) * 6
-                    to = u * 12 + h * 6
-                    row_out[o][zl, to:to + 6, :] = block[at:at + 6, h * LANES:(h + 1) * LANES].astype(bf16)
-        xb = (x_at ^ o) * 16
-        for q in range(4):
-            w, h = wide[q]
-            a = slab_c[pl.ds(pl.multiple_of(xb + w * 64, 8), 16), h * LANES:(h + 1) * LANES]
-            w, h = slim[q]
-            e = slab_c[pl.ds(pl.multiple_of(xb + w * 64, 8), 16), h * LANES:(h + 1) * LANES]
-            even, odd = e[:8], e[8:]
-            if q % 2 == 0:
-                b = jnp.where(low, even, pltpu.roll(odd, 64, 1))
-            else:
-                b = jnp.where(low, pltpu.roll(even, 64, 1), odd)
-            col_out[o][q, 0:16, :] = a.astype(bf16)
-            col_out[o][q, 16:24, :] = b.astype(bf16)
+    core = lax.axis_index("k")
+
+    def put_rows(out):
+        for o in range(4):
+            block = slab_f[pl.ds(pl.multiple_of((y_at ^ o) * 48, 8), 48), :]
+            for zl in range(4):
+                for u in range(2):
+                    for h in range(2):
+                        at = (zl * 2 + u) * 6
+                        to = u * 12 + h * 6
+                        out[o * 4 + zl, to:to + 6, :] = block[at:at + 6, h * LANES:(h + 1) * LANES].astype(bf16)
+
+    def put_cols(out):
+        for o in range(4):
+            xb = (x_at ^ o) * 16
+            for q in range(4):
+                w, h = wide[q]
+                a = slab_c[pl.ds(pl.multiple_of(xb + w * 64, 8), 16), h * LANES:(h + 1) * LANES]
+                w, h = slim[q]
+                e = slab_c[pl.ds(pl.multiple_of(xb + w * 64, 8), 16), h * LANES:(h + 1) * LANES]
+                even, odd = e[:8], e[8:]
+                if q % 2 == 0:
+                    b = jnp.where(low, even, pltpu.roll(odd, 64, 1))
+                else:
+                    b = jnp.where(low, pltpu.roll(even, 64, 1), odd)
+                out[o * 4 + q, 0:16, :] = a.astype(bf16)
+                out[o * 4 + q, 16:24, :] = b.astype(bf16)
+
+    @pl.when(core == 0)
+    def _():
+        put_rows(keep)
+        put_cols(give)
+
+    @pl.when(core == 1)
+    def _():
+        put_cols(keep)
+        put_rows(give)
 
 
 def vmem(shape, dtype=jnp.bfloat16):
@@ -139,41 +152,87 @@
 def front(fields, phase):
     return pl.pallas_call(
         front_kernel,
-        out_shape=[vmem((4, ROWS, LANES))] * 8,
-        out_specs=[pl.BlockSpec(memory_space=pltpu.VMEM)] * 8,
+        out_shape=[vmem((16, ROWS, LANES))] * 2,
+        out_specs=[pl.BlockSpec(memory_space=pltpu.VMEM)] * 2,
         scratch_shapes=[pltpu.VMEM((192, NY), jnp.float32), pltpu.VMEM((192, NY), jnp.float32)],
         name="front",
     )(fields, phase, *tables())
 
 
-def pack_kernel(*refs):
-    rows = refs[:4]
-    cols = refs[4:8]
-    outs = refs[8:]
+def lay_kernel(keep, got, *outs):
+    is_first = lax.axis_index("k") == 0
+
+    @pl.when(is_first)
+    def _():
+        for o, out in enumerate(outs):
+            out[0:4] = keep[o * 4:o * 4 + 4]
+            out[4:8] = got[o * 4:o * 4 + 4]
+
+    @pl.when(jnp.logical_not(is_first))
+    def _():
+        for o, out in enumerate(outs):
+            out[0:4] = got[o * 4:o * 4 + 4]
+            out[4:8] = keep[o * 4:o * 4 + 4]
+
+
+def lay(keep, got):
+    return local_call(lay_kernel, [(8, ROWS, LANES)] * 4, [keep, got])
+
+
+def stack_kernel(*refs):
+    out = refs[4]
+    for o in range(4):
+        out[o * 8:o * 8 + 8] = refs[o][...]
+
+
+def stack(parts):
+    return local_call(stack_kernel, [(32, ROWS, LANES)], parts)[0]
+
+
+def pack_kernel(mine, other, z1, z2, z3, z4, home):
+    core = lax.axis_index("k")
     z_at = lax.axis_index("zh") * 4 + lax.axis_index("zl")
-    for d, out in enumerate(outs):
-        z = (z_at + d) % 8
+
+    def fill(out, z, rows, cols, electrons):
         zh = z // 4
         zl = z % 4
-        for o in range(4):
-            for k in range(2):
-                to = o * 48 + k * 24
-                out[to:to + 24, :] = cols[o][zh * 2 + k]
-            to = 192 + o * 24
-            out[to:to + 24, :] = rows[o][zl]
-
-
-def pack(rows, cols):
-    return local_call(pack_kernel, [(PEER_ROWS, LANES)] * 8, [*rows, *cols])
+        for i, e in enumerate(electrons):
+            for o in range(4):
+                at = (o * 2 + e) * 4
+                for k in range(2):
+                    to = i * PEER_ROWS + o * 48 + k * 24
+                    out[to:to + 24, :] = cols[at + zh * 2 + k]
+                to = i * PEER_ROWS + 192 + o * 24
+                out[to:to + 24, :] = rows[at + zl]
+
+    def fill_all(rows, cols, sign, e):
+        for d, out in ((1, z1), (2, z2), (3, z3)):
+            fill(out, (z_at + sign * d + 8) % 8, rows, cols, (0, 1))
+        fill(z4, (z_at + 4) % 8, rows, cols, (e,))
+        fill(home, z_at, rows, cols, (e,))
+
+    @pl.when(core == 0)
+    def _():
+        fill_all(mine, other, 1, 0)
+
+    @pl.when(core == 1)
+    def _():
+        fill_all(other, mine, -1, 1)
+
+
+def pack(mine, other):
+    return local_call(pack_kernel, [(2 * PEER_ROWS, LANES)] * 3 + [(PEER_ROWS, LANES)] * 2, [mine, other])
 
 
 def split_kernel(*refs):
-    peers = refs[:8]
-    mine, theirs, flat = refs[8:]
+    peers = refs[:5]
+    mine, theirs, flat = refs[5:]
     bf16 = jnp.bfloat16
     core = lax.axis_index("k")
-    for z in range(8):
-        flat[z * PEER_ROWS:(z + 1) * PEER_ROWS, :] = peers[z][...].astype(jnp.float32)
+    at = 0
+    for peer in peers:
+        flat[at:at + peer.shape[0], :] = peer[...].astype(jnp.float32)
+        at += peer.shape[0]
 
     def pair(at, step):
         return jnp.concatenate(
@@ -193,10 +252,7 @@
 
 def split(peers):
     return local_call(
-        split_kernel,
-        [(18, 64, LANES)] * 2,
-        peers,
-        scratch=[pltpu.VMEM((8 * PEER_ROWS, LANES), jnp.float32)],
+        split_kernel, [(18, 64, LANES)] * 2, peers, scratch=[pltpu.VMEM((8 * PEER_ROWS, LANES), jnp.float32)]
     )
 
 
@@ -314,18 +370,37 @@
     return lax.ppermute(value, axis, [(i, i ^ bits) for i in range(lax.axis_size(axis))])
 
 
-def shift(value, by):
-    return lax.ppermute(value, ("zh", "zl"), [(i, (i + by) % 8) for i in range(8)])
+def coordinates(device):
+    return dict(x=device % 4, y=device // 4 % 4, z=device // 16 % 4 + device // 128 * 4, k=device // 64 % 2)
+
+
+def move(value, change):
+    pairs = []
+    for device in range(256):
+        at = coordinates(device)
+        to = {**at, **change(**at)}
+        pairs.append((device, (((to["z"] // 4 * 2 + to["k"]) * 4 + to["z"] % 4) * 4 + to["y"]) * 4 + to["x"]))
+    return lax.ppermute(value, AXES, pairs)
 
 
 def body(fields, mirror_phase, tile_list):
-    pieces = front(fields, mirror_phase)
-    rows, cols = pieces[:4], pieces[4:]
-    cols = [cols[0]] + [swap(cols[o], "x", o) for o in (1, 2, 3)]
-    rows = [rows[0]] + [swap(rows[o], "y", o) for o in (1, 2, 3)]
-    peers = pack(rows, cols)
-    peers = [peers[0]] + [shift(peers[o], o) for o in range(1, 8)]
-    mine, theirs = split(peers)
+    keep, give = front(fields, mirror_phase)
+    got = swap(give, "k", 1)
+    parts = lay(keep, got)
+
+    def scatter(o):
+        return lambda x, y, k, **at: {"y": y ^ o} if k == 0 else {"x": x ^ o}
+
+    parts = [parts[0]] + [move(parts[o], scatter(o)) for o in (1, 2, 3)]
+    mine = stack(parts)
+    other = swap(mine, "k", 1)
+
+    def along(d):
+        return lambda z, k, **at: {"z": (z + (d if k == 0 else -d)) % 8}
+
+    z1, z2, z3, z4, home = pack(mine, other)
+    z1, z2, z3, z4 = [move(v, along(d)) for d, v in ((1, z1), (2, z2), (3, z3), (4, z4))]
+    mine, theirs = split([z1, z2, z3, home, z4])
     theirs = swap(theirs, "k", 1)
     r0, c0 = merge(mine, theirs)
     c1 = swap(c0, "y", 1)

time: 87.7 us -> 82.8 us (0.944)
  starting transfers between devices: 34.3 us -> 31.2 us
  waiting for transfers between devices: 40.3 us -> 38.3 us
    ppermute x15 -> x11, waiting for transfers between devices: 31.8 us -> 29.4 us  [swap(): lax.ppermute(value, axis, [(i, i ^ bits) for i in range(lax.axis_size(axi...]
    ppermute x15 -> x11, starting transfers between devices: 17.8 us -> 15.5 us  [swap(): lax.ppermute(value, axis, [(i, i ^ bits) for i in range(lax.axis_size(axi...]
  transfers between devices with their start and end apart: 22 -> 18, of which waited for: 12 -> 12; matrix products, arithmetic and copies ran while one was open for 1% -> 1% of each run, Pallas kernels for 0% -> 0%
where the time goes in v1:
time: 82.8 us; the launch traced here: 82.5 us
  waiting for transfers between devices  38.3 us (46%)
  starting transfers between devices  31.2 us (38%)
  Pallas kernels  11.9 us (14%)
    ppermute x11, waiting for transfers between devices, swap(): lax.ppermute(value, axis, [(i, i ^ bits) for i in range(lax.axis_size(axi...  29.4 us
    ppermute x7, starting transfers between devices, move(): return lax.ppermute(value, AXES, pairs)  15.7 us
    ppermute x11, starting transfers between devices, swap(): lax.ppermute(value, axis, [(i, i ^ bits) for i in range(lax.axis_size(axi...  15.5 us
    ppermute x7, waiting for transfers between devices, move(): return lax.ppermute(value, AXES, pairs)  8.96 us
    pallas_call x1, Pallas kernels, back(): pl.pallas_call(back_kernel, in_specs=[pl.BlockSpec(memory_space=pltpu.SME...  6.88 us
    pallas_call x1, Pallas kernels, front(): pl.pallas_call(front_kernel, out_shape=[vmem((16, ROWS, LANES))] * 2, out...  4.01 us
  transfers between devices with their start and end apart: 18, of which 12 were waited for; matrix products, arithmetic and copies ran while one was open for 1% of the time, Pallas kernels for 0%

profile of v1, /device:TPU:1, one launch (start us, length us, event | category | flops | bytes accessed | tf_op | source)
XLA Modules:
  0.0 82.5 jit_solution(9787752788056665552)
XLA Ops:
  0.0 4.0 %front.1 = (bf16[16,24,128]{2,1,0:T(8,128)(2,1)S(1)}, bf16[16,24,128]{2,1,0:T(8,128)(2,1)S(1)}) custom-call(bf16[1,2,512,256]{3,2,1,0:T(8,128)(2,1)} %fields.1, f32[512,256]{1,0:T(8,128)} %phase.1, bf16[512,512]{1,0:T(8,128)(2,1)} %constant.14.clone.cos_x, bf16[512,512]{1,0:T(8,128)(2,1)} %constant.15.clone.sin_x, bf16[256,256]{1,0:T(8,128)(2,1)} %constant.16.clone.cos_y, ...), custom_call_target="tpu_custom_call" | custom-call | tf_op jit(solution)/shard_map/front/pallas_call | solution.py:153
  4.0 3.3 %collective-permute-start = (bf16[16,24,128]{2,1,0:T(8,128)(2,1)S(1)}, bf16[16,24,128]{2,1,0:T(8,128)(2,1)S(1)}, u32[]{:S(2)}, u32[]{:S(2)}) collective-permute-start(bf16[16,24,128]{2,1,0:T(8,128)(2,1)S(1)} %get-tuple-element.21), channel_id=1, source_target_pairs={{0,64},{64,0},{1,65},{65,1},{2,66},{66,2},{3,67},{67,3},{4,68},{68... | collective-permute-start | bytes 294920 | tf_op jit(solution)/shard_map/ppermute | solution.py:370
  7.3 0.9 %collective-permute-done.got = bf16[16,24,128]{2,1,0:T(8,128)(2,1)S(1)} collective-permute-done((bf16[16,24,128]{2,1,0:T(8,128)(2,1)S(1)}, bf16[16,24,128]{2,1,0:T(8,128)(2,1)S(1)}, u32[]{:S(2)}, u32[]{:S(2)}) %collective-permute-start) | collective-permute-done | bytes 98336 | tf_op jit(solution)/shard_map/ppermute | solution.py:370
  8.3 0.1 collective-permute-start.1
  8.4 1.9 %collective-permute-start.2 = (bf16[8,24,128]{2,1,0:T(8,128)(2,1)S(1)}, bf16[8,24,128]{2,1,0:T(8,128)(2,1)S(1)}, u32[]{:S(2)}, u32[]{:S(2)}) collective-permute-start(bf16[8,24,128]{2,1,0:T(8,128)(2,1)S(1)} %get-tuple-element.24), channel_id=1, source_target_pairs={{0,8},{1,9},{2,10},{3,11},{4,12},{5,13},{6,14},{7,15},{8,0},{9,1},... | collective-permute-start | bytes 147464 | tf_op jit(solution)/shard_map/ppermute | solution.py:383
  10.3 1.9 %collective-permute-start.3 = (bf16[8,24,128]{2,1,0:T(8,128)(2,1)S(1)}, bf16[8,24,128]{2,1,0:T(8,128)(2,1)S(1)}, u32[]{:S(2)}, u32[]{:S(2)}) collective-permute-start(bf16[8,24,128]{2,1,0:T(8,128)(2,1)S(1)} %get-tuple-element.25), channel_id=1, source_target_pairs={{0,12},{1,13},{2,14},{3,15},{4,8},{5,9},{6,10},{7,11},{8,4},{9,5},... | collective-permute-start | bytes 147464 | tf_op jit(solution)/shard_map/ppermute | solution.py:383
  12.2 0.0 collective-permute-done.1.refs_1_
  12.2 0.7 collective-permute-done.2.refs_2_
  12.9 1.6 %collective-permute-done.3.refs_3_ = bf16[8,24,128]{2,1,0:T(8,128)(2,1)S(1)} collective-permute-done((bf16[8,24,128]{2,1,0:T(8,128)(2,1)S(1)}, bf16[8,24,128]{2,1,0:T(8,128)(2,1)S(1)}, u32[]{:S(2)}, u32[]{:S(2)}) %collective-permute-start.3) | collective-permute-done | bytes 49184 | tf_op jit(solution)/shard_map/ppermute | solution.py:383
  14.5 2.4 %collective-permute-start.4 = (bf16[32,24,128]{2,1,0:T(8,128)(2,1)S(1)}, bf16[32,24,128]{2,1,0:T(8,128)(2,1)S(1)}, u32[]{:S(2)}, u32[]{:S(2)}) collective-permute-start(bf16[32,24,128]{2,1,0:T(8,128)(2,1)S(1)} %shard_map.101.mine), channel_id=1, source_target_pairs={{0,64},{64,0},{1,65},{65,1},{2,66},{66,2},{3,67},{67,3},{4,68},{68... | collective-permute-start | bytes 589832 | tf_op jit(solution)/shard_map/ppermute | solution.py:370
  16.9 1.1 %collective-permute-done.4.other = bf16[32,24,128]{2,1,0:T(8,128)(2,1)S(1)} collective-permute-done((bf16[32,24,128]{2,1,0:T(8,128)(2,1)S(1)}, bf16[32,24,128]{2,1,0:T(8,128)(2,1)S(1)}, u32[]{:S(2)}, u32[]{:S(2)}) %collective-permute-start.4) | collective-permute-done | bytes 196640 | tf_op jit(solution)/shard_map/ppermute | solution.py:370
  18.0 5.6 %collective-permute-start.5 = (bf16[576,128]{1,0:T(8,128)(2,1)S(1)}, bf16[576,128]{1,0:T(8,128)(2,1)S(1)}, u32[]{:S(2)}, u32[]{:S(2)}) collective-permute-start(bf16[576,128]{1,0:T(8,128)(2,1)S(1)} %get-tuple-element.26), channel_id=1, source_target_pairs={{0,16},{1,17},{2,18},{3,19},{4,20},{5,21},{6,22},{7,23},{8,24},{9,... | collective-permute-start | bytes 442376 | tf_op jit(solution)/shard_map/ppermute | solution.py:383
  23.7 1.2 %collective-permute-start.6 = (bf16[576,128]{1,0:T(8,128)(2,1)S(1)}, bf16[576,128]{1,0:T(8,128)(2,1)S(1)}, u32[]{:S(2)}, u32[]{:S(2)}) collective-permute-start(bf16[576,128]{1,0:T(8,128)(2,1)S(1)} %get-tuple-element.27), channel_id=1, source_target_pairs={{0,32},{1,33},{2,34},{3,35},{4,36},{5,37},{6,38},{7,39},{8,40},{9,... | collective-permute-start | bytes 442376 | tf_op jit(solution)/shard_map/ppermute | solution.py:383
  24.8 0.5 collective-permute-start.7
  25.3 4.5 %collective-permute-start.8 = (bf16[288,128]{1,0:T(8,128)(2,1)S(1)}, bf16[288,128]{1,0:T(8,128)(2,1)S(1)}, u32[]{:S(2)}, u32[]{:S(2)}) collective-permute-start(bf16[288,128]{1,0:T(8,128)(2,1)S(1)} %get-tuple-element.30), channel_id=1, source_target_pairs={{0,128},{1,129},{2,130},{3,131},{4,132},{5,133},{6,134},{7,135},{8... | collective-permute-start | bytes 221192 | tf_op jit(solution)/shard_map/ppermute | solution.py:383
  29.8 6.7 %collective-permute-done.8.refs_4_ = bf16[288,128]{1,0:T(8,128)(2,1)S(1)} collective-permute-done((bf16[288,128]{1,0:T(8,128)(2,1)S(1)}, bf16[288,128]{1,0:T(8,128)(2,1)S(1)}, u32[]{:S(2)}, u32[]{:S(2)}) %collective-permute-start.8) | collective-permute-done | bytes 73760 | tf_op jit(solution)/shard_map/ppermute | solution.py:383
  36.5 0.0 collective-permute-done.5.refs_0_
  36.5 0.0 collective-permute-done.6.refs_1_
  36.5 0.0 collective-permute-done.7.refs_2_
  36.5 0.7 shard_map.103
  37.2 3.2 %collective-permute-start.9 = (bf16[18,64,128]{2,1,0:T(8,128)(2,1)S(1)}, bf16[18,64,128]{2,1,0:T(8,128)(2,1)S(1)}, u32[]{:S(2)}, u32[]{:S(2)}) collective-permute-start(bf16[18,64,128]{2,1,0:T(8,128)(2,1)S(1)} %get-tuple-element.32), channel_id=1, source_target_pairs={{0,64},{64,0},{1,65},{65,1},{2,66},{66,2},{3,67},{67,3},{4,68},{68... | collective-permute-start | bytes 884744 | tf_op jit(solution)/shard_map/ppermute | solution.py:370
  40.5 1.2 %collective-permute-done.9.theirs = bf16[18,64,128]{2,1,0:T(8,128)(2,1)S(1)} collective-permute-done((bf16[18,64,128]{2,1,0:T(8,128)(2,1)S(1)}, bf16[18,64,128]{2,1,0:T(8,128)(2,1)S(1)}, u32[]{:S(2)}, u32[]{:S(2)}) %collective-permute-start.9) | collective-permute-done | bytes 294944 | tf_op jit(solution)/shard_map/ppermute | solution.py:370
  41.7 0.2 shard_map.104
  41.9 2.6 %collective-permute-start.11 = (bf16[128,768]{1,0:T(8,128)(2,1)S(1)}, bf16[128,768]{1,0:T(8,128)(2,1)S(1)}, u32[]{:S(2)}, u32[]{:S(2)}) collective-permute-start(bf16[128,768]{1,0:T(8,128)(2,1)S(1)} %get-tuple-element.33.r0), channel_id=1, source_target_pairs={{0,3},{1,2},{2,1},{3,0},{4,7},{5,6},{6,5},{7,4},{8,11},{9,10},{10,... | collective-permute-start | bytes 589832 | tf_op jit(solution)/shard_map/ppermute | solution.py:370
  44.4 0.0 collective-permute-start.10
  44.4 4.8 %collective-permute-done.11.r3 = bf16[128,768]{1,0:T(8,128)(2,1)S(1)} collective-permute-done((bf16[128,768]{1,0:T(8,128)(2,1)S(1)}, bf16[128,768]{1,0:T(8,128)(2,1)S(1)}, u32[]{:S(2)}, u32[]{:S(2)}) %collective-permute-start.11) | collective-permute-done | bytes 196640 | tf_op jit(solution)/shard_map/ppermute | solution.py:370
  49.2 0.0 collective-permute-start.12
  49.2 1.0 %collective-permute-done.10.r1 = bf16[128,768]{1,0:T(8,128)(2,1)S(1)} collective-permute-done((bf16[128,768]{1,0:T(8,128)(2,1)S(1)}, bf16[128,768]{1,0:T(8,128)(2,1)S(1)}, u32[]{:S(2)}, u32[]{:S(2)}) %collective-permute-start.10) | collective-permute-done | bytes 196640 | tf_op jit(solution)/shard_map/ppermute | solution.py:370
  50.2 4.2 %collective-permute-done.12.r2 = bf16[128,768]{1,0:T(8,128)(2,1)S(1)} collective-permute-done((bf16[128,768]{1,0:T(8,128)(2,1)S(1)}, bf16[128,768]{1,0:T(8,128)(2,1)S(1)}, u32[]{:S(2)}, u32[]{:S(2)}) %collective-permute-start.12) | collective-permute-done | bytes 196640 | tf_op jit(solution)/shard_map/ppermute | solution.py:370
  54.5 0.1 shard_map.105.own
  54.5 2.2 %collective-permute-start.13 = (bf16[512,768]{1,0:T(8,128)(2,1)S(1)}, bf16[512,768]{1,0:T(8,128)(2,1)S(1)}, u32[]{:S(2)}, u32[]{:S(2)}) collective-permute-start(bf16[512,768]{1,0:T(8,128)(2,1)S(1)} %shard_map.105.own), channel_id=1, source_target_pairs={{0,64},{64,0},{1,65},{65,1},{2,66},{66,2},{3,67},{67,3},{4,68},{68... | collective-permute-start | bytes 2359304 | tf_op jit(solution)/shard_map/ppermute | solution.py:370
  56.7 0.6 collective-permute-start.15
  57.3 0.0 collective-permute-start.14
  57.3 11.2 %collective-permute-done.15.c3 = bf16[12,128,128]{2,1,0:T(8,128)(2,1)S(1)} collective-permute-done((bf16[12,128,128]{2,1,0:T(8,128)(2,1)S(1)}, bf16[12,128,128]{2,1,0:T(8,128)(2,1)S(1)}, u32[]{:S(2)}, u32[]{:S(2)}) %collective-permute-start.15) | collective-permute-done | bytes 393248 | tf_op jit(solution)/shard_map/ppermute | solution.py:370
  68.5 0.1 collective-permute-start.16
  68.6 0.0 collective-permute-done.14.c1
  68.6 1.1 %collective-permute-start.17 = (bf16[6,128,128]{2,1,0:T(8,128)(2,1)S(1)}, bf16[6,128,128]{2,1,0:T(8,128)(2,1)S(1)}, u32[]{:S(2)}, u32[]{:S(2)}) collective-permute-start(bf16[6,128,128]{2,1,0:T(8,128)(2,1)S(1)} %slice.9), channel_id=1, source_target_pairs={{0,12},{4,8},{8,4},{12,0},{1,13},{5,9},{9,5},{13,1},{2,14},{6,10},... | collective-permute-start | bytes 589832 | tf_op jit(solution)/shard_map/ppermute | solution.py:370
  69.8 0.8 copy.11.tiles
  70.5 3.5 %collective-permute-done.16.c2a = bf16[6,128,128]{2,1,0:T(8,128)(2,1)S(1)} collective-permute-done((bf16[6,128,128]{2,1,0:T(8,128)(2,1)S(1)}, bf16[6,128,128]{2,1,0:T(8,128)(2,1)S(1)}, u32[]{:S(2)}, u32[]{:S(2)}) %collective-permute-start.16) | collective-permute-done | bytes 196640 | tf_op jit(solution)/shard_map/ppermute | solution.py:370
  74.1 1.3 %collective-permute-done.17.c2b = bf16[6,128,128]{2,1,0:T(8,128)(2,1)S(1)} collective-permute-done((bf16[6,128,128]{2,1,0:T(8,128)(2,1)S(1)}, bf16[6,128,128]{2,1,0:T(8,128)(2,1)S(1)}, u32[]{:S(2)}, u32[]{:S(2)}) %collective-permute-start.17) | collective-permute-done | bytes 196640 | tf_op jit(solution)/shard_map/ppermute | solution.py:370
  75.4 0.0 collective-permute-done.13.other
  75.4 6.9 %back.1 = f32[1,1,9,2,192,768]{5,4,3,2,1,0:T(8,128)} custom-call(s32[1,1,9,2]{3,2,1,0:T(8,128)S(1)} %copy.11.tiles, bf16[512,768]{1,0:T(8,128)(2,1)S(1)} %shard_map.105.own, bf16[512,768]{1,0:T(8,128)(2,1)S(1)} %collective-permute-done.13.other, bf16[12,128,128]{2,1,0:T(8,128)(2,1)S(1)} %get-tuple-element.34.c0, ...), custom_call_target="tpu_custom_call" | custom-call | tf_op jit(solution)/shard_map/back/pallas_call | solution.py:354
  (5 shorter events, 0.1 us)
Async XLA Ops:
  4.0 4.2 %collective-permute-start = (bf16[16,24,128]{2,1,0:T(8,128)(2,1)S(1)}, bf16[16,24,128]{2,1,0:T(8,128)(2,1)S(1)}, u32[]{:S(2)}, u32[]{:S(2)}) collective-permute-start(bf16[16,24,128]{2,1,0:T(8,128)(2,1)S(1)} %get-tuple-element.21), channel_id=1, source_target_pairs={{0,64},{64,0},{1,65},{65,1},{2,66},{66,2},{3,67},{67,3},{4,68},{68... | collective-permute-start | bytes 294920 | tf_op jit(solution)/shard_map/ppermute | solution.py:370
  8.3 3.9 %collective-permute-start.1 = (bf16[8,24,128]{2,1,0:T(8,128)(2,1)S(1)}, bf16[8,24,128]{2,1,0:T(8,128)(2,1)S(1)}, u32[]{:S(2)}, u32[]{:S(2)}) collective-permute-start(bf16[8,24,128]{2,1,0:T(8,128)(2,1)S(1)} %get-tuple-element.23), channel_id=1, source_target_pairs={{0,4},{1,5},{2,6},{3,7},{4,0},{5,1},{6,2},{7,3},{8,12},{9,13},{10,... | collective-permute-start | bytes 147464 | tf_op jit(solution)/shard_map/ppermute | solution.py:383
  8.4 4.5 %collective-permute-start.2 = (bf16[8,24,128]{2,1,0:T(8,128)(2,1)S(1)}, bf16[8,24,128]{2,1,0:T(8,128)(2,1)S(1)}, u32[]{:S(2)}, u32[]{:S(2)}) collective-permute-start(bf16[8,24,128]{2,1,0:T(8,128)(2,1)S(1)} %get-tuple-element.24), channel_id=1, source_target_pairs={{0,8},{1,9},{2,10},{3,11},{4,12},{5,13},{6,14},{7,15},{8,0},{9,1},... | collective-permute-start | bytes 147464 | tf_op jit(solution)/shard_map/ppermute | solution.py:383
  10.3 4.2 %collective-permute-start.3 = (bf16[8,24,128]{2,1,0:T(8,128)(2,1)S(1)}, bf16[8,24,128]{2,1,0:T(8,128)(2,1)S(1)}, u32[]{:S(2)}, u32[]{:S(2)}) collective-permute-start(bf16[8,24,128]{2,1,0:T(8,128)(2,1)S(1)} %get-tuple-element.25), channel_id=1, source_target_pairs={{0,12},{1,13},{2,14},{3,15},{4,8},{5,9},{6,10},{7,11},{8,4},{9,5},... | collective-permute-start | bytes 147464 | tf_op jit(solution)/shard_map/ppermute | solution.py:383
  14.5 3.5 %collective-permute-start.4 = (bf16[32,24,128]{2,1,0:T(8,128)(2,1)S(1)}, bf16[32,24,128]{2,1,0:T(8,128)(2,1)S(1)}, u32[]{:S(2)}, u32[]{:S(2)}) collective-permute-start(bf16[32,24,128]{2,1,0:T(8,128)(2,1)S(1)} %shard_map.101.mine), channel_id=1, source_target_pairs={{0,64},{64,0},{1,65},{65,1},{2,66},{66,2},{3,67},{67,3},{4,68},{68... | collective-permute-start | bytes 589832 | tf_op jit(solution)/shard_map/ppermute | solution.py:370
  18.0 18.5 %collective-permute-start.5 = (bf16[576,128]{1,0:T(8,128)(2,1)S(1)}, bf16[576,128]{1,0:T(8,128)(2,1)S(1)}, u32[]{:S(2)}, u32[]{:S(2)}) collective-permute-start(bf16[576,128]{1,0:T(8,128)(2,1)S(1)} %get-tuple-element.26), channel_id=1, source_target_pairs={{0,16},{1,17},{2,18},{3,19},{4,20},{5,21},{6,22},{7,23},{8,24},{9,... | collective-permute-start | bytes 442376 | tf_op jit(solution)/shard_map/ppermute | solution.py:383
  23.7 12.8 %collective-permute-start.6 = (bf16[576,128]{1,0:T(8,128)(2,1)S(1)}, bf16[576,128]{1,0:T(8,128)(2,1)S(1)}, u32[]{:S(2)}, u32[]{:S(2)}) collective-permute-start(bf16[576,128]{1,0:T(8,128)(2,1)S(1)} %get-tuple-element.27), channel_id=1, source_target_pairs={{0,32},{1,33},{2,34},{3,35},{4,36},{5,37},{6,38},{7,39},{8,40},{9,... | collective-permute-start | bytes 442376 | tf_op jit(solution)/shard_map/ppermute | solution.py:383
  24.8 11.7 %collective-permute-start.7 = (bf16[576,128]{1,0:T(8,128)(2,1)S(1)}, bf16[576,128]{1,0:T(8,128)(2,1)S(1)}, u32[]{:S(2)}, u32[]{:S(2)}) collective-permute-start(bf16[576,128]{1,0:T(8,128)(2,1)S(1)} %get-tuple-element.28), channel_id=1, source_target_pairs={{0,48},{1,49},{2,50},{3,51},{4,52},{5,53},{6,54},{7,55},{8,56},{9,... | collective-permute-start | bytes 442376 | tf_op jit(solution)/shard_map/ppermute | solution.py:383
  25.3 11.2 %collective-permute-start.8 = (bf16[288,128]{1,0:T(8,128)(2,1)S(1)}, bf16[288,128]{1,0:T(8,128)(2,1)S(1)}, u32[]{:S(2)}, u32[]{:S(2)}) collective-permute-start(bf16[288,128]{1,0:T(8,128)(2,1)S(1)} %get-tuple-element.30), channel_id=1, source_target_pairs={{0,128},{1,129},{2,130},{3,131},{4,132},{5,133},{6,134},{7,135},{8... | collective-permute-start | bytes 221192 | tf_op jit(solution)/shard_map/ppermute | solution.py:383
  37.2 4.4 %collective-permute-start.9 = (bf16[18,64,128]{2,1,0:T(8,128)(2,1)S(1)}, bf16[18,64,128]{2,1,0:T(8,128)(2,1)S(1)}, u32[]{:S(2)}, u32[]{:S(2)}) collective-permute-start(bf16[18,64,128]{2,1,0:T(8,128)(2,1)S(1)} %get-tuple-element.32), channel_id=1, source_target_pairs={{0,64},{64,0},{1,65},{65,1},{2,66},{66,2},{3,67},{67,3},{4,68},{68... | collective-permute-start | bytes 884744 | tf_op jit(solution)/shard_map/ppermute | solution.py:370
  41.9 7.4 %collective-permute-start.11 = (bf16[128,768]{1,0:T(8,128)(2,1)S(1)}, bf16[128,768]{1,0:T(8,128)(2,1)S(1)}, u32[]{:S(2)}, u32[]{:S(2)}) collective-permute-start(bf16[128,768]{1,0:T(8,128)(2,1)S(1)} %get-tuple-element.33.r0), channel_id=1, source_target_pairs={{0,3},{1,2},{2,1},{3,0},{4,7},{5,6},{6,5},{7,4},{8,11},{9,10},{10,... | collective-permute-start | bytes 589832 | tf_op jit(solution)/shard_map/ppermute | solution.py:370
  44.4 5.8 %collective-permute-start.10 = (bf16[128,768]{1,0:T(8,128)(2,1)S(1)}, bf16[128,768]{1,0:T(8,128)(2,1)S(1)}, u32[]{:S(2)}, u32[]{:S(2)}) collective-permute-start(bf16[128,768]{1,0:T(8,128)(2,1)S(1)} %get-tuple-element.33.r0), channel_id=1, source_target_pairs={{0,1},{1,0},{2,3},{3,2},{4,5},{5,4},{6,7},{7,6},{8,9},{9,8},{10,11... | collective-permute-start | bytes 589832 | tf_op jit(solution)/shard_map/ppermute | solution.py:370
  49.2 5.2 %collective-permute-start.12 = (bf16[128,768]{1,0:T(8,128)(2,1)S(1)}, bf16[128,768]{1,0:T(8,128)(2,1)S(1)}, u32[]{:S(2)}, u32[]{:S(2)}) collective-permute-start(bf16[128,768]{1,0:T(8,128)(2,1)S(1)} %collective-permute-done.11.r3), channel_id=1, source_target_pairs={{0,1},{1,0},{2,3},{3,2},{4,5},{5,4},{6,7},{7,6},{8,9},{9,8},{10,11... | collective-permute-start | bytes 589832 | tf_op jit(solution)/shard_map/ppermute | solution.py:370
  54.5 20.9 %collective-permute-start.13 = (bf16[512,768]{1,0:T(8,128)(2,1)S(1)}, bf16[512,768]{1,0:T(8,128)(2,1)S(1)}, u32[]{:S(2)}, u32[]{:S(2)}) collective-permute-start(bf16[512,768]{1,0:T(8,128)(2,1)S(1)} %shard_map.105.own), channel_id=1, source_target_pairs={{0,64},{64,0},{1,65},{65,1},{2,66},{66,2},{3,67},{67,3},{4,68},{68... | collective-permute-start | bytes 2359304 | tf_op jit(solution)/shard_map/ppermute | solution.py:370
  56.7 11.8 %collective-permute-start.15 = (bf16[12,128,128]{2,1,0:T(8,128)(2,1)S(1)}, bf16[12,128,128]{2,1,0:T(8,128)(2,1)S(1)}, u32[]{:S(2)}, u32[]{:S(2)}) collective-permute-start(bf16[12,128,128]{2,1,0:T(8,128)(2,1)S(1)} %get-tuple-element.34.c0), channel_id=1, source_target_pairs={{0,12},{4,8},{8,4},{12,0},{1,13},{5,9},{9,5},{13,1},{2,14},{6,10},... | collective-permute-start | bytes 1179656 | tf_op jit(solution)/shard_map/ppermute | solution.py:370
  57.3 11.3 %collective-permute-start.14 = (bf16[12,128,128]{2,1,0:T(8,128)(2,1)S(1)}, bf16[12,128,128]{2,1,0:T(8,128)(2,1)S(1)}, u32[]{:S(2)}, u32[]{:S(2)}) collective-permute-start(bf16[12,128,128]{2,1,0:T(8,128)(2,1)S(1)} %get-tuple-element.34.c0), channel_id=1, source_target_pairs={{0,4},{4,0},{8,12},{12,8},{1,5},{5,1},{9,13},{13,9},{2,6},{6,2},{1... | collective-permute-start | bytes 1179656 | tf_op jit(solution)/shard_map/ppermute | solution.py:370
  68.5 5.6 %collective-permute-start.16 = (bf16[6,128,128]{2,1,0:T(8,128)(2,1)S(1)}, bf16[6,128,128]{2,1,0:T(8,128)(2,1)S(1)}, u32[]{:S(2)}, u32[]{:S(2)}) collective-permute-start(bf16[6,128,128]{2,1,0:T(8,128)(2,1)S(1)} %slice.8), channel_id=1, source_target_pairs={{0,4},{4,0},{8,12},{12,8},{1,5},{5,1},{9,13},{13,9},{2,6},{6,2},{1... | collective-permute-start | bytes 589832 | tf_op jit(solution)/shard_map/ppermute | solution.py:370
  68.6 6.8 %collective-permute-start.17 = (bf16[6,128,128]{2,1,0:T(8,128)(2,1)S(1)}, bf16[6,128,128]{2,1,0:T(8,128)(2,1)S(1)}, u32[]{:S(2)}, u32[]{:S(2)}) collective-permute-start(bf16[6,128,128]{2,1,0:T(8,128)(2,1)S(1)} %slice.9), channel_id=1, source_target_pairs={{0,12},{4,8},{8,4},{12,0},{1,13},{5,9},{9,5},{13,1},{2,14},{6,10},... | collective-permute-start | bytes 589832 | tf_op jit(solution)/shard_map/ppermute | solution.py:370

commit v2 on v1

--- a/solution.py
+++ b/solution.py
@@ -289,7 +289,9 @@
     return local_call(join_kernel, [(512, TILE)], blocks)[0]
 
 
-def back_kernel(tiles, own, other, c0, c1, c2a, c2b, c3, out, left, ready, sem):
+def back_kernel(tiles, own, other, c0, c1, c2a, c2b, c3, out, left, ready, right, sem):
+    right[0] = own[...]
+    right[1] = other[...]
     core = lax.axis_index("k")
     wide_at = pl.multiple_of(core * 64, 64)
     slim_at = pl.multiple_of((1 - core) * 128, 64)
@@ -323,27 +325,14 @@
         m = jnp.maximum(tile_col, 0) // 4
         u = (tile_row >= 16).astype(jnp.int32)
 
-        def write(right):
-            res = dot(left[m], right[...]) * 0.0625
-            ready[slot, 0] = res[:QUARTER]
-            ready[slot, 1] = res[QUARTER:]
-
-        @pl.when(jnp.logical_and(tile_row >= 0, u == core))
-        def _():
-            write(own)
-
-        @pl.when(jnp.logical_and(tile_row >= 0, u != core))
-        def _():
-            write(other)
-
-        @pl.when(tile_row < 0)
-        def _():
-            ready[slot] = jnp.zeros((2, QUARTER, TILE), jnp.float32)
-
+        scale = jnp.where(tile_row >= 0, 0.0625, 0.0)
+        res = dot(left[m], right[jnp.where(u == core, 0, 1)]) * scale
+        ready[slot, 0] = res[:QUARTER]
+        ready[slot, 1] = res[QUARTER:]
         copy(slot).start()
         return carry
 
-    lax.fori_loop(0, SLOTS, one, 0)
+    lax.fori_loop(0, SLOTS, one, 0, unroll=3)
     for slot in range(SLOTS):
         copy(slot).wait()
 
@@ -358,6 +347,7 @@
         scratch_shapes=[
             pltpu.VMEM((8, 2 * QUARTER, 512), jnp.bfloat16),
             pltpu.VMEM((SLOTS, 2, QUARTER, TILE), jnp.float32),
+            pltpu.VMEM((2, 512, TILE), jnp.bfloat16),
             pltpu.SemaphoreType.DMA((SLOTS,)),
         ],
         compiler_params=pltpu.CompilerParams(vmem_limit_bytes=28 << 20),

time: 82.8 us -> 82.1 us (level)
    pallas_call x1, Pallas kernels: 6.88 us -> 6.02 us  [back(): pl.pallas_call(back_kernel, in_specs=[pl.BlockSpec(memory_space=pltpu.SME...]
where the time goes in v2:
time: 82.1 us; the launch traced here: 81.6 us
  waiting for transfers between devices  38.3 us (47%)
  starting transfers between devices  31.2 us (38%)
  Pallas kernels  11.1 us (14%)
    ppermute x11, waiting for transfers between devices, swap(): lax.ppermute(value, axis, [(i, i ^ bits) for i in range(lax.axis_size(axi...  29.4 us
    ppermute x7, starting transfers between devices, move(): return lax.ppermute(value, AXES, pairs)  15.7 us
    ppermute x11, starting transfers between devices, swap(): lax.ppermute(value, axis, [(i, i ^ bits) for i in range(lax.axis_size(axi...  15.5 us
    ppermute x7, waiting for transfers between devices, move(): return lax.ppermute(value, AXES, pairs)  8.96 us
    pallas_call x1, Pallas kernels, back(): pl.pallas_call(back_kernel, in_specs=[pl.BlockSpec(memory_space=pltpu.SME...  6.02 us
    pallas_call x1, Pallas kernels, front(): pl.pallas_call(front_kernel, out_shape=[vmem((16, ROWS, LANES))] * 2, out...  4.01 us
  transfers between devices with their start and end apart: 18, of which 12 were waited for; matrix products, arithmetic and copies ran while one was open for 1% of the time, Pallas kernels for 0%

profile of v2, /device:TPU:1, one launch (start us, length us, event | category | flops | bytes accessed | tf_op | source)
XLA Modules:
  0.0 81.6 jit_solution(11530172127863229182)
XLA Ops:
  0.0 4.0 %front.1 = (bf16[16,24,128]{2,1,0:T(8,128)(2,1)S(1)}, bf16[16,24,128]{2,1,0:T(8,128)(2,1)S(1)}) custom-call(bf16[1,2,512,256]{3,2,1,0:T(8,128)(2,1)} %fields.1, f32[512,256]{1,0:T(8,128)} %phase.1, bf16[512,512]{1,0:T(8,128)(2,1)} %constant.14.clone.cos_x, bf16[512,512]{1,0:T(8,128)(2,1)} %constant.15.clone.sin_x, bf16[256,256]{1,0:T(8,128)(2,1)} %constant.16.clone.cos_y, ...), custom_call_target="tpu_custom_call" | custom-call | tf_op jit(solution)/shard_map/front/pallas_call | solution.py:153
  4.0 3.3 %collective-permute-start = (bf16[16,24,128]{2,1,0:T(8,128)(2,1)S(1)}, bf16[16,24,128]{2,1,0:T(8,128)(2,1)S(1)}, u32[]{:S(2)}, u32[]{:S(2)}) collective-permute-start(bf16[16,24,128]{2,1,0:T(8,128)(2,1)S(1)} %get-tuple-element.21), channel_id=1, source_target_pairs={{0,64},{64,0},{1,65},{65,1},{2,66},{66,2},{3,67},{67,3},{4,68},{68... | collective-permute-start | bytes 294920 | tf_op jit(solution)/shard_map/ppermute | solution.py:360
  7.3 0.9 %collective-permute-done.got = bf16[16,24,128]{2,1,0:T(8,128)(2,1)S(1)} collective-permute-done((bf16[16,24,128]{2,1,0:T(8,128)(2,1)S(1)}, bf16[16,24,128]{2,1,0:T(8,128)(2,1)S(1)}, u32[]{:S(2)}, u32[]{:S(2)}) %collective-permute-start) | collective-permute-done | bytes 98336 | tf_op jit(solution)/shard_map/ppermute | solution.py:360
  8.3 0.1 collective-permute-start.1
  8.4 1.9 %collective-permute-start.2 = (bf16[8,24,128]{2,1,0:T(8,128)(2,1)S(1)}, bf16[8,24,128]{2,1,0:T(8,128)(2,1)S(1)}, u32[]{:S(2)}, u32[]{:S(2)}) collective-permute-start(bf16[8,24,128]{2,1,0:T(8,128)(2,1)S(1)} %get-tuple-element.24), channel_id=1, source_target_pairs={{0,8},{1,9},{2,10},{3,11},{4,12},{5,13},{6,14},{7,15},{8,0},{9,1},... | collective-permute-start | bytes 147464 | tf_op jit(solution)/shard_map/ppermute | solution.py:373
  10.3 1.9 %collective-permute-start.3 = (bf16[8,24,128]{2,1,0:T(8,128)(2,1)S(1)}, bf16[8,24,128]{2,1,0:T(8,128)(2,1)S(1)}, u32[]{:S(2)}, u32[]{:S(2)}) collective-permute-start(bf16[8,24,128]{2,1,0:T(8,128)(2,1)S(1)} %get-tuple-element.25), channel_id=1, source_target_pairs={{0,12},{1,13},{2,14},{3,15},{4,8},{5,9},{6,10},{7,11},{8,4},{9,5},... | collective-permute-start | bytes 147464 | tf_op jit(solution)/shard_map/ppermute | solution.py:373
  12.2 0.0 collective-permute-done.1.refs_1_
  12.2 0.7 collective-permute-done.2.refs_2_
  12.9 1.6 %collective-permute-done.3.refs_3_ = bf16[8,24,128]{2,1,0:T(8,128)(2,1)S(1)} collective-permute-done((bf16[8,24,128]{2,1,0:T(8,128)(2,1)S(1)}, bf16[8,24,128]{2,1,0:T(8,128)(2,1)S(1)}, u32[]{:S(2)}, u32[]{:S(2)}) %collective-permute-start.3) | collective-permute-done | bytes 49184 | tf_op jit(solution)/shard_map/ppermute | solution.py:373
  14.5 2.4 %collective-permute-start.4 = (bf16[32,24,128]{2,1,0:T(8,128)(2,1)S(1)}, bf16[32,24,128]{2,1,0:T(8,128)(2,1)S(1)}, u32[]{:S(2)}, u32[]{:S(2)}) collective-permute-start(bf16[32,24,128]{2,1,0:T(8,128)(2,1)S(1)} %shard_map.101.mine), channel_id=1, source_target_pairs={{0,64},{64,0},{1,65},{65,1},{2,66},{66,2},{3,67},{67,3},{4,68},{68... | collective-permute-start | bytes 589832 | tf_op jit(solution)/shard_map/ppermute | solution.py:360
  16.9 1.1 %collective-permute-done.4.other = bf16[32,24,128]{2,1,0:T(8,128)(2,1)S(1)} collective-permute-done((bf16[32,24,128]{2,1,0:T(8,128)(2,1)S(1)}, bf16[32,24,128]{2,1,0:T(8,128)(2,1)S(1)}, u32[]{:S(2)}, u32[]{:S(2)}) %collective-permute-start.4) | collective-permute-done | bytes 196640 | tf_op jit(solution)/shard_map/ppermute | solution.py:360
  18.0 5.6 %collective-permute-start.5 = (bf16[576,128]{1,0:T(8,128)(2,1)S(1)}, bf16[576,128]{1,0:T(8,128)(2,1)S(1)}, u32[]{:S(2)}, u32[]{:S(2)}) collective-permute-start(bf16[576,128]{1,0:T(8,128)(2,1)S(1)} %get-tuple-element.26), channel_id=1, source_target_pairs={{0,16},{1,17},{2,18},{3,19},{4,20},{5,21},{6,22},{7,23},{8,24},{9,... | collective-permute-start | bytes 442376 | tf_op jit(solution)/shard_map/ppermute | solution.py:373
  23.7 1.2 %collective-permute-start.6 = (bf16[576,128]{1,0:T(8,128)(2,1)S(1)}, bf16[576,128]{1,0:T(8,128)(2,1)S(1)}, u32[]{:S(2)}, u32[]{:S(2)}) collective-permute-start(bf16[576,128]{1,0:T(8,128)(2,1)S(1)} %get-tuple-element.27), channel_id=1, source_target_pairs={{0,32},{1,33},{2,34},{3,35},{4,36},{5,37},{6,38},{7,39},{8,40},{9,... | collective-permute-start | bytes 442376 | tf_op jit(solution)/shard_map/ppermute | solution.py:373
  24.8 0.5 collective-permute-start.7
  25.3 4.5 %collective-permute-start.8 = (bf16[288,128]{1,0:T(8,128)(2,1)S(1)}, bf16[288,128]{1,0:T(8,128)(2,1)S(1)}, u32[]{:S(2)}, u32[]{:S(2)}) collective-permute-start(bf16[288,128]{1,0:T(8,128)(2,1)S(1)} %get-tuple-element.30), channel_id=1, source_target_pairs={{0,128},{1,129},{2,130},{3,131},{4,132},{5,133},{6,134},{7,135},{8... | collective-permute-start | bytes 221192 | tf_op jit(solution)/shard_map/ppermute | solution.py:373
  29.8 6.7 %collective-permute-done.8.refs_4_ = bf16[288,128]{1,0:T(8,128)(2,1)S(1)} collective-permute-done((bf16[288,128]{1,0:T(8,128)(2,1)S(1)}, bf16[288,128]{1,0:T(8,128)(2,1)S(1)}, u32[]{:S(2)}, u32[]{:S(2)}) %collective-permute-start.8) | collective-permute-done | bytes 73760 | tf_op jit(solution)/shard_map/ppermute | solution.py:373
  36.5 0.0 collective-permute-done.5.refs_0_
  36.5 0.0 collective-permute-done.6.refs_1_
  36.5 0.0 collective-permute-done.7.refs_2_
  36.5 0.7 shard_map.103
  37.2 3.2 %collective-permute-start.9 = (bf16[18,64,128]{2,1,0:T(8,128)(2,1)S(1)}, bf16[18,64,128]{2,1,0:T(8,128)(2,1)S(1)}, u32[]{:S(2)}, u32[]{:S(2)}) collective-permute-start(bf16[18,64,128]{2,1,0:T(8,128)(2,1)S(1)} %get-tuple-element.32), channel_id=1, source_target_pairs={{0,64},{64,0},{1,65},{65,1},{2,66},{66,2},{3,67},{67,3},{4,68},{68... | collective-permute-start | bytes 884744 | tf_op jit(solution)/shard_map/ppermute | solution.py:360
  40.5 1.2 %collective-permute-done.9.theirs = bf16[18,64,128]{2,1,0:T(8,128)(2,1)S(1)} collective-permute-done((bf16[18,64,128]{2,1,0:T(8,128)(2,1)S(1)}, bf16[18,64,128]{2,1,0:T(8,128)(2,1)S(1)}, u32[]{:S(2)}, u32[]{:S(2)}) %collective-permute-start.9) | collective-permute-done | bytes 294944 | tf_op jit(solution)/shard_map/ppermute | solution.py:360
  41.7 0.2 shard_map.104
  41.9 2.6 %collective-permute-start.11 = (bf16[128,768]{1,0:T(8,128)(2,1)S(1)}, bf16[128,768]{1,0:T(8,128)(2,1)S(1)}, u32[]{:S(2)}, u32[]{:S(2)}) collective-permute-start(bf16[128,768]{1,0:T(8,128)(2,1)S(1)} %get-tuple-element.33.r0), channel_id=1, source_target_pairs={{0,3},{1,2},{2,1},{3,0},{4,7},{5,6},{6,5},{7,4},{8,11},{9,10},{10,... | collective-permute-start | bytes 589832 | tf_op jit(solution)/shard_map/ppermute | solution.py:360
  44.4 0.0 collective-permute-start.10
  44.4 4.8 %collective-permute-done.11.r3 = bf16[128,768]{1,0:T(8,128)(2,1)S(1)} collective-permute-done((bf16[128,768]{1,0:T(8,128)(2,1)S(1)}, bf16[128,768]{1,0:T(8,128)(2,1)S(1)}, u32[]{:S(2)}, u32[]{:S(2)}) %collective-permute-start.11) | collective-permute-done | bytes 196640 | tf_op jit(solution)/shard_map/ppermute | solution.py:360
  49.2 0.0 collective-permute-start.12
  49.2 1.0 %collective-permute-done.10.r1 = bf16[128,768]{1,0:T(8,128)(2,1)S(1)} collective-permute-done((bf16[128,768]{1,0:T(8,128)(2,1)S(1)}, bf16[128,768]{1,0:T(8,128)(2,1)S(1)}, u32[]{:S(2)}, u32[]{:S(2)}) %collective-permute-start.10) | collective-permute-done | bytes 196640 | tf_op jit(solution)/shard_map/ppermute | solution.py:360
  50.2 4.2 %collective-permute-done.12.r2 = bf16[128,768]{1,0:T(8,128)(2,1)S(1)} collective-permute-done((bf16[128,768]{1,0:T(8,128)(2,1)S(1)}, bf16[128,768]{1,0:T(8,128)(2,1)S(1)}, u32[]{:S(2)}, u32[]{:S(2)}) %collective-permute-start.12) | collective-permute-done | bytes 196640 | tf_op jit(solution)/shard_map/ppermute | solution.py:360
  54.5 0.1 shard_map.105.own
  54.5 2.2 %collective-permute-start.13 = (bf16[512,768]{1,0:T(8,128)(2,1)S(1)}, bf16[512,768]{1,0:T(8,128)(2,1)S(1)}, u32[]{:S(2)}, u32[]{:S(2)}) collective-permute-start(bf16[512,768]{1,0:T(8,128)(2,1)S(1)} %shard_map.105.own), channel_id=1, source_target_pairs={{0,64},{64,0},{1,65},{65,1},{2,66},{66,2},{3,67},{67,3},{4,68},{68... | collective-permute-start | bytes 2359304 | tf_op jit(solution)/shard_map/ppermute | solution.py:360
  56.7 0.6 collective-permute-start.15
  57.3 0.0 collective-permute-start.14
  57.3 11.2 %collective-permute-done.15.c3 = bf16[12,128,128]{2,1,0:T(8,128)(2,1)S(1)} collective-permute-done((bf16[12,128,128]{2,1,0:T(8,128)(2,1)S(1)}, bf16[12,128,128]{2,1,0:T(8,128)(2,1)S(1)}, u32[]{:S(2)}, u32[]{:S(2)}) %collective-permute-start.15) | collective-permute-done | bytes 393248 | tf_op jit(solution)/shard_map/ppermute | solution.py:360
  68.5 0.1 collective-permute-start.16
  68.6 0.0 collective-permute-done.14.c1
  68.6 1.1 %collective-permute-start.17 = (bf16[6,128,128]{2,1,0:T(8,128)(2,1)S(1)}, bf16[6,128,128]{2,1,0:T(8,128)(2,1)S(1)}, u32[]{:S(2)}, u32[]{:S(2)}) collective-permute-start(bf16[6,128,128]{2,1,0:T(8,128)(2,1)S(1)} %slice.9), channel_id=1, source_target_pairs={{0,12},{4,8},{8,4},{12,0},{1,13},{5,9},{9,5},{13,1},{2,14},{6,10},... | collective-permute-start | bytes 589832 | tf_op jit(solution)/shard_map/ppermute | solution.py:360
  69.8 0.8 copy.11.tiles
  70.5 3.5 %collective-permute-done.16.c2a = bf16[6,128,128]{2,1,0:T(8,128)(2,1)S(1)} collective-permute-done((bf16[6,128,128]{2,1,0:T(8,128)(2,1)S(1)}, bf16[6,128,128]{2,1,0:T(8,128)(2,1)S(1)}, u32[]{:S(2)}, u32[]{:S(2)}) %collective-permute-start.16) | collective-permute-done | bytes 196640 | tf_op jit(solution)/shard_map/ppermute | solution.py:360
  74.1 1.3 %collective-permute-done.17.c2b = bf16[6,128,128]{2,1,0:T(8,128)(2,1)S(1)} collective-permute-done((bf16[6,128,128]{2,1,0:T(8,128)(2,1)S(1)}, bf16[6,128,128]{2,1,0:T(8,128)(2,1)S(1)}, u32[]{:S(2)}, u32[]{:S(2)}) %collective-permute-start.17) | collective-permute-done | bytes 196640 | tf_op jit(solution)/shard_map/ppermute | solution.py:360
  75.4 0.0 collective-permute-done.13.other
  75.4 6.0 %back.1 = f32[1,1,9,2,192,768]{5,4,3,2,1,0:T(8,128)} custom-call(s32[1,1,9,2]{3,2,1,0:T(8,128)S(1)} %copy.11.tiles, bf16[512,768]{1,0:T(8,128)(2,1)S(1)} %shard_map.105.own, bf16[512,768]{1,0:T(8,128)(2,1)S(1)} %collective-permute-done.13.other, bf16[12,128,128]{2,1,0:T(8,128)(2,1)S(1)} %get-tuple-element.34.c0, ...), custom_call_target="tpu_custom_call" | custom-call | tf_op jit(solution)/shard_map/back/pallas_call | solution.py:343
  (5 shorter events, 0.1 us)
Async XLA Ops:
  4.0 4.2 %collective-permute-start = (bf16[16,24,128]{2,1,0:T(8,128)(2,1)S(1)}, bf16[16,24,128]{2,1,0:T(8,128)(2,1)S(1)}, u32[]{:S(2)}, u32[]{:S(2)}) collective-permute-start(bf16[16,24,128]{2,1,0:T(8,128)(2,1)S(1)} %get-tuple-element.21), channel_id=1, source_target_pairs={{0,64},{64,0},{1,65},{65,1},{2,66},{66,2},{3,67},{67,3},{4,68},{68... | collective-permute-start | bytes 294920 | tf_op jit(solution)/shard_map/ppermute | solution.py:360
  8.3 3.9 %collective-permute-start.1 = (bf16[8,24,128]{2,1,0:T(8,128)(2,1)S(1)}, bf16[8,24,128]{2,1,0:T(8,128)(2,1)S(1)}, u32[]{:S(2)}, u32[]{:S(2)}) collective-permute-start(bf16[8,24,128]{2,1,0:T(8,128)(2,1)S(1)} %get-tuple-element.23), channel_id=1, source_target_pairs={{0,4},{1,5},{2,6},{3,7},{4,0},{5,1},{6,2},{7,3},{8,12},{9,13},{10,... | collective-permute-start | bytes 147464 | tf_op jit(solution)/shard_map/ppermute | solution.py:373
  8.4 4.5 %collective-permute-start.2 = (bf16[8,24,128]{2,1,0:T(8,128)(2,1)S(1)}, bf16[8,24,128]{2,1,0:T(8,128)(2,1)S(1)}, u32[]{:S(2)}, u32[]{:S(2)}) collective-permute-start(bf16[8,24,128]{2,1,0:T(8,128)(2,1)S(1)} %get-tuple-element.24), channel_id=1, source_target_pairs={{0,8},{1,9},{2,10},{3,11},{4,12},{5,13},{6,14},{7,15},{8,0},{9,1},... | collective-permute-start | bytes 147464 | tf_op jit(solution)/shard_map/ppermute | solution.py:373
  10.3 4.2 %collective-permute-start.3 = (bf16[8,24,128]{2,1,0:T(8,128)(2,1)S(1)}, bf16[8,24,128]{2,1,0:T(8,128)(2,1)S(1)}, u32[]{:S(2)}, u32[]{:S(2)}) collective-permute-start(bf16[8,24,128]{2,1,0:T(8,128)(2,1)S(1)} %get-tuple-element.25), channel_id=1, source_target_pairs={{0,12},{1,13},{2,14},{3,15},{4,8},{5,9},{6,10},{7,11},{8,4},{9,5},... | collective-permute-start | bytes 147464 | tf_op jit(solution)/shard_map/ppermute | solution.py:373
  14.5 3.5 %collective-permute-start.4 = (bf16[32,24,128]{2,1,0:T(8,128)(2,1)S(1)}, bf16[32,24,128]{2,1,0:T(8,128)(2,1)S(1)}, u32[]{:S(2)}, u32[]{:S(2)}) collective-permute-start(bf16[32,24,128]{2,1,0:T(8,128)(2,1)S(1)} %shard_map.101.mine), channel_id=1, source_target_pairs={{0,64},{64,0},{1,65},{65,1},{2,66},{66,2},{3,67},{67,3},{4,68},{68... | collective-permute-start | bytes 589832 | tf_op jit(solution)/shard_map/ppermute | solution.py:360
  18.0 18.5 %collective-permute-start.5 = (bf16[576,128]{1,0:T(8,128)(2,1)S(1)}, bf16[576,128]{1,0:T(8,128)(2,1)S(1)}, u32[]{:S(2)}, u32[]{:S(2)}) collective-permute-start(bf16[576,128]{1,0:T(8,128)(2,1)S(1)} %get-tuple-element.26), channel_id=1, source_target_pairs={{0,16},{1,17},{2,18},{3,19},{4,20},{5,21},{6,22},{7,23},{8,24},{9,... | collective-permute-start | bytes 442376 | tf_op jit(solution)/shard_map/ppermute | solution.py:373
  23.7 12.8 %collective-permute-start.6 = (bf16[576,128]{1,0:T(8,128)(2,1)S(1)}, bf16[576,128]{1,0:T(8,128)(2,1)S(1)}, u32[]{:S(2)}, u32[]{:S(2)}) collective-permute-start(bf16[576,128]{1,0:T(8,128)(2,1)S(1)} %get-tuple-element.27), channel_id=1, source_target_pairs={{0,32},{1,33},{2,34},{3,35},{4,36},{5,37},{6,38},{7,39},{8,40},{9,... | collective-permute-start | bytes 442376 | tf_op jit(solution)/shard_map/ppermute | solution.py:373
  24.8 11.7 %collective-permute-start.7 = (bf16[576,128]{1,0:T(8,128)(2,1)S(1)}, bf16[576,128]{1,0:T(8,128)(2,1)S(1)}, u32[]{:S(2)}, u32[]{:S(2)}) collective-permute-start(bf16[576,128]{1,0:T(8,128)(2,1)S(1)} %get-tuple-element.28), channel_id=1, source_target_pairs={{0,48},{1,49},{2,50},{3,51},{4,52},{5,53},{6,54},{7,55},{8,56},{9,... | collective-permute-start | bytes 442376 | tf_op jit(solution)/shard_map/ppermute | solution.py:373
  25.3 11.2 %collective-permute-start.8 = (bf16[288,128]{1,0:T(8,128)(2,1)S(1)}, bf16[288,128]{1,0:T(8,128)(2,1)S(1)}, u32[]{:S(2)}, u32[]{:S(2)}) collective-permute-start(bf16[288,128]{1,0:T(8,128)(2,1)S(1)} %get-tuple-element.30), channel_id=1, source_target_pairs={{0,128},{1,129},{2,130},{3,131},{4,132},{5,133},{6,134},{7,135},{8... | collective-permute-start | bytes 221192 | tf_op jit(solution)/shard_map/ppermute | solution.py:373
  37.2 4.4 %collective-permute-start.9 = (bf16[18,64,128]{2,1,0:T(8,128)(2,1)S(1)}, bf16[18,64,128]{2,1,0:T(8,128)(2,1)S(1)}, u32[]{:S(2)}, u32[]{:S(2)}) collective-permute-start(bf16[18,64,128]{2,1,0:T(8,128)(2,1)S(1)} %get-tuple-element.32), channel_id=1, source_target_pairs={{0,64},{64,0},{1,65},{65,1},{2,66},{66,2},{3,67},{67,3},{4,68},{68... | collective-permute-start | bytes 884744 | tf_op jit(solution)/shard_map/ppermute | solution.py:360
  41.9 7.4 %collective-permute-start.11 = (bf16[128,768]{1,0:T(8,128)(2,1)S(1)}, bf16[128,768]{1,0:T(8,128)(2,1)S(1)}, u32[]{:S(2)}, u32[]{:S(2)}) collective-permute-start(bf16[128,768]{1,0:T(8,128)(2,1)S(1)} %get-tuple-element.33.r0), channel_id=1, source_target_pairs={{0,3},{1,2},{2,1},{3,0},{4,7},{5,6},{6,5},{7,4},{8,11},{9,10},{10,... | collective-permute-start | bytes 589832 | tf_op jit(solution)/shard_map/ppermute | solution.py:360
  44.4 5.8 %collective-permute-start.10 = (bf16[128,768]{1,0:T(8,128)(2,1)S(1)}, bf16[128,768]{1,0:T(8,128)(2,1)S(1)}, u32[]{:S(2)}, u32[]{:S(2)}) collective-permute-start(bf16[128,768]{1,0:T(8,128)(2,1)S(1)} %get-tuple-element.33.r0), channel_id=1, source_target_pairs={{0,1},{1,0},{2,3},{3,2},{4,5},{5,4},{6,7},{7,6},{8,9},{9,8},{10,11... | collective-permute-start | bytes 589832 | tf_op jit(solution)/shard_map/ppermute | solution.py:360
  49.2 5.2 %collective-permute-start.12 = (bf16[128,768]{1,0:T(8,128)(2,1)S(1)}, bf16[128,768]{1,0:T(8,128)(2,1)S(1)}, u32[]{:S(2)}, u32[]{:S(2)}) collective-permute-start(bf16[128,768]{1,0:T(8,128)(2,1)S(1)} %collective-permute-done.11.r3), channel_id=1, source_target_pairs={{0,1},{1,0},{2,3},{3,2},{4,5},{5,4},{6,7},{7,6},{8,9},{9,8},{10,11... | collective-permute-start | bytes 589832 | tf_op jit(solution)/shard_map/ppermute | solution.py:360
  54.5 20.9 %collective-permute-start.13 = (bf16[512,768]{1,0:T(8,128)(2,1)S(1)}, bf16[512,768]{1,0:T(8,128)(2,1)S(1)}, u32[]{:S(2)}, u32[]{:S(2)}) collective-permute-start(bf16[512,768]{1,0:T(8,128)(2,1)S(1)} %shard_map.105.own), channel_id=1, source_target_pairs={{0,64},{64,0},{1,65},{65,1},{2,66},{66,2},{3,67},{67,3},{4,68},{68... | collective-permute-start | bytes 2359304 | tf_op jit(solution)/shard_map/ppermute | solution.py:360
  56.7 11.8 %collective-permute-start.15 = (bf16[12,128,128]{2,1,0:T(8,128)(2,1)S(1)}, bf16[12,128,128]{2,1,0:T(8,128)(2,1)S(1)}, u32[]{:S(2)}, u32[]{:S(2)}) collective-permute-start(bf16[12,128,128]{2,1,0:T(8,128)(2,1)S(1)} %get-tuple-element.34.c0), channel_id=1, source_target_pairs={{0,12},{4,8},{8,4},{12,0},{1,13},{5,9},{9,5},{13,1},{2,14},{6,10},... | collective-permute-start | bytes 1179656 | tf_op jit(solution)/shard_map/ppermute | solution.py:360
  57.3 11.3 %collective-permute-start.14 = (bf16[12,128,128]{2,1,0:T(8,128)(2,1)S(1)}, bf16[12,128,128]{2,1,0:T(8,128)(2,1)S(1)}, u32[]{:S(2)}, u32[]{:S(2)}) collective-permute-start(bf16[12,128,128]{2,1,0:T(8,128)(2,1)S(1)} %get-tuple-element.34.c0), channel_id=1, source_target_pairs={{0,4},{4,0},{8,12},{12,8},{1,5},{5,1},{9,13},{13,9},{2,6},{6,2},{1... | collective-permute-start | bytes 1179656 | tf_op jit(solution)/shard_map/ppermute | solution.py:360
  68.5 5.6 %collective-permute-start.16 = (bf16[6,128,128]{2,1,0:T(8,128)(2,1)S(1)}, bf16[6,128,128]{2,1,0:T(8,128)(2,1)S(1)}, u32[]{:S(2)}, u32[]{:S(2)}) collective-permute-start(bf16[6,128,128]{2,1,0:T(8,128)(2,1)S(1)} %slice.8), channel_id=1, source_target_pairs={{0,4},{4,0},{8,12},{12,8},{1,5},{5,1},{9,13},{13,9},{2,6},{6,2},{1... | collective-permute-start | bytes 589832 | tf_op jit(solution)/shard_map/ppermute | solution.py:360
  68.6 6.8 %collective-permute-start.17 = (bf16[6,128,128]{2,1,0:T(8,128)(2,1)S(1)}, bf16[6,128,128]{2,1,0:T(8,128)(2,1)S(1)}, u32[]{:S(2)}, u32[]{:S(2)}) collective-permute-start(bf16[6,128,128]{2,1,0:T(8,128)(2,1)S(1)} %slice.9), channel_id=1, source_target_pairs={{0,12},{4,8},{8,4},{12,0},{1,13},{5,9},{9,5},{13,1},{2,14},{6,10},... | collective-permute-start | bytes 589832 | tf_op jit(solution)/shard_map/ppermute | solution.py:360
